TPU v7x, 256 devices: a whole 4x4x8 slice. The times are simulated.
256 devices in a mesh: group: 4 (over x_hi, core), tensor: 64 (over x_lo, y, z).
Axes of the slice: x: 4 (x_hi: 2, x_lo: 2; x = x_hi * 2 + x_lo), y: 4, z: 8, core: 2. Of those that a mesh axis runs over, the one named last changes fastest.
Arguments:
- hidden_in: bfloat16 [8192, 2048], P('tensor'), may hold values from -6 to 6
- queries: bfloat16 [8192, 3072], P('tensor', 'group'), may hold values from -10 to 10
- suffix_latent: bfloat16 [8192, 576], P('tensor'), may hold values from -10 to 10
- prefix_latent: bfloat16 [2048, 576], P(('group', 'tensor')), may hold values from -6 to 6
- key_up: bfloat16 [16, 128, 512], P('group'), may hold values from -0.5 to 0.5
- value_up: bfloat16 [16, 512, 128], P('group'), may hold values from -0.25 to 0.25
- output_weight: bfloat16 [2048, 2048], P('group'), may hold values from -0.125 to 0.125
- norm_gain: bfloat16 [2048], replicated, may hold values from 0.5 to 1.5
- router: bfloat16 [2048, 64], replicated, may hold values from -0.125 to 0.125
- expert_gate: bfloat16 [64, 2048, 1408], P('tensor', None, 'group'), may hold values from -0.125 to 0.125
- expert_up: bfloat16 [64, 2048, 1408], P('tensor', None, 'group'), may hold values from -0.125 to 0.125
- expert_down: bfloat16 [64, 1408, 2048], P('tensor', 'group'), may hold values from -0.15625 to 0.15625
- next_gain: bfloat16 [2048], replicated, may hold values from 0.5 to 1.5
- next_query_weight: bfloat16 [2048, 3072], P(None, 'group'), may hold values from -0.125 to 0.125
- next_latent_weight: bfloat16 [2048, 576], P(None, 'group'), may hold values from -0.125 to 0.125
- suffix_lengths: int32 [32], replicated, may hold values from 1 to 513, 8192 in all
- request_tenant: int32 [32], replicated, may hold values from 0 to 3
- tenant_lengths: int32 [4], replicated, may hold values from 1 to 1024, 2048 in all
- page_table: int32 [256], replicated, may hold values from 0 to 255, each once
- routes: int32 [4, 2048, 6], P(None, 'tensor'), may hold values from 0 to 63, all different within a row; in each aligned block of 32 rows (0 to 31, 32 to 63, ..., all dimensions but the last counted through in order) at most 4 rows name the same one
Outputs:
- layer_out: bfloat16 [2048, 4, 2048], P('tensor', 'group')
- next_queries: bfloat16 [8192, 3072], P('tensor', 'group')
- next_latent: bfloat16 [8192, 576], P('tensor', 'group')
Inputs may be any that keep to these rules, and one draw needn't show every extreme that they name: `page_table`: each stored page maps to a different logical page. In each aligned block of 32 rows of routes (in its order g, a) an expert is named by at most 4 rows, and some block reaches 4; the 6 experts of a token differ.
All inputs are finite; a program needn't handle non-finite values.
Results may differ from a plain program's by a relative error of at most 0.018.
Values may be sent and summed in bfloat16 or wider, within the bound.
A program may use at most 128 MiB of HBM per device.

v0:
```python
import math

import jax
import jax.numpy as jnp
from jax import lax
from jax.sharding import PartitionSpec as P

NOPE = 128
ROPE = 64
LAT = 512
PAGE = 8
REACH = 4


VERY_NEGATIVE = -1e30
ROUTE_SCALING = 2.446
NORM_EPSILON = 1e-06


def shifted(block, axis, distance):
    devices = range(lax.axis_size(axis))
    route = [(i - distance, i) for i in devices if i - distance in devices]
    return lax.ppermute(block, axis, route)


def norm_rows(row_block, gain_vector):
    values = row_block.astype(jnp.float32)
    mean_square = jnp.mean(values * values, axis=-1, keepdims=True)
    return (
        values * lax.rsqrt(mean_square + NORM_EPSILON) * gain_vector.astype(jnp.float32)
    ).astype(jnp.bfloat16)


def attend_block(running, query_rows, key_rows, visible, heads_dev, score_scale):
    best_score, weight_sum, accumulated = running
    token_count = visible.shape[0]
    scores = jnp.einsum("rc,kc->rk", query_rows, key_rows, preferred_element_type=jnp.float32)
    scores = scores.reshape(token_count, heads_dev, -1) * score_scale
    masked = jnp.where(visible[:, None, :], scores, VERY_NEGATIVE)
    new_best = jnp.maximum(best_score, jnp.max(masked, axis=-1))
    weights = jnp.where(visible[:, None, :], jnp.exp(masked - new_best[:, :, None]), 0.0)
    factor = jnp.exp(best_score - new_best)
    weight_sum = weight_sum * factor + jnp.sum(weights, axis=-1)
    rounded = weights.astype(jnp.bfloat16).reshape(token_count * heads_dev, -1)
    update = jnp.dot(rounded, key_rows[:, :LAT], preferred_element_type=jnp.float32)
    accumulated = accumulated * factor[:, :, None] + update.reshape(token_count, heads_dev, -1)
    return (new_best, weight_sum, accumulated)


def route_weights(normed, router, route_ids):
    probs = jax.nn.sigmoid(jnp.dot(normed, router, preferred_element_type=jnp.float32))
    picked = jnp.take_along_axis(probs, route_ids, axis=1)
    return picked / jnp.sum(picked, axis=1, keepdims=True) * ROUTE_SCALING


def slot_targets(route_ids, expert_count, capacity):
    flat_ids = route_ids.reshape(-1)
    hit_table = (flat_ids[:, None] == jnp.arange(expert_count, dtype=jnp.int32)[None, :]).astype(
        jnp.int32
    )
    rank_table = jnp.cumsum(hit_table, axis=0) - hit_table
    slot_index = jnp.sum(rank_table * hit_table, axis=1)
    return (flat_ids * capacity + slot_index).reshape(route_ids.shape)


def pack_rows(normed, targets, slots_total):
    select = jnp.any(
        jnp.arange(slots_total, dtype=jnp.int32)[:, None, None] == targets[None, :, :], axis=2
    )
    return jnp.dot(select.astype(jnp.bfloat16), normed, preferred_element_type=jnp.float32).astype(
        jnp.bfloat16
    )


def expert_apply(row_block, gate_part, up_part, down_part):
    lead_shape = row_block.shape[:-1]
    flat_rows = row_block.reshape(-1, row_block.shape[-1])
    gate_vals = jnp.dot(flat_rows, gate_part, preferred_element_type=jnp.float32)
    up_vals = jnp.dot(flat_rows, up_part, preferred_element_type=jnp.float32)
    hidden_vals = (jax.nn.silu(gate_vals) * up_vals).astype(jnp.bfloat16)
    output_rows = jnp.dot(hidden_vals, down_part, preferred_element_type=jnp.float32).astype(
        jnp.bfloat16
    )
    return output_rows.reshape(lead_shape + (down_part.shape[1],))


def per_device(
    hidden_in,
    queries,
    suffix_latent,
    prefix_latent,
    key_up,
    value_up,
    output_weight,
    norm_gain,
    router,
    expert_gate,
    expert_up,
    expert_down,
    next_gain,
    next_query_weight,
    next_latent_weight,
    suffix_lengths,
    request_tenant,
    tenant_lengths,
    page_table,
    routes,
):
    tok_slice = hidden_in.shape[0]
    width = hidden_in.shape[1]
    heads_dev = key_up.shape[0]
    groups = lax.axis_size("group")
    group_index = lax.axis_index("group")
    tensor_index = lax.axis_index("tensor")
    tok_quarter = tok_slice // groups
    key_width = suffix_latent.shape[1]
    expert_count = router.shape[1]
    top_count = routes.shape[2]
    score_scale = 1.0 / math.sqrt(NOPE + ROPE)
    first_token = tensor_index * tok_slice
    positions = first_token + jnp.arange(tok_slice, dtype=jnp.int32)
    request_ends = jnp.cumsum(suffix_lengths)
    request_starts = request_ends - suffix_lengths
    inside = (positions[:, None] >= request_starts[None, :]) & (
        positions[:, None] < request_ends[None, :]
    )
    token_start = jnp.sum(jnp.where(inside, request_starts[None, :], 0), axis=1)
    token_tenant = jnp.sum(jnp.where(inside, request_tenant[None, :], 0), axis=1)
    tenant_ends = jnp.cumsum(tenant_lengths)
    tenant_starts = tenant_ends - tenant_lengths
    tenant_pick = (
        token_tenant[:, None] == jnp.arange(tenant_lengths.shape[0], dtype=jnp.int32)[None, :]
    )
    range_low = jnp.sum(jnp.where(tenant_pick, tenant_starts[None, :], 0), axis=1)
    range_high = jnp.sum(jnp.where(tenant_pick, tenant_ends[None, :], 0), axis=1)
    page_count = page_table.shape[0]
    query_split = queries.reshape(tok_slice, heads_dev, NOPE + ROPE)
    absorbed = jnp.einsum(
        "thn,hnl->thl", query_split[:, :, :NOPE], key_up, preferred_element_type=jnp.float32
    ).astype(jnp.bfloat16)
    query_rows = jnp.concatenate([absorbed, query_split[:, :, NOPE:]], axis=-1).reshape(
        tok_slice * heads_dev, key_width
    )
    start_state = (
        jnp.full((tok_slice, heads_dev), VERY_NEGATIVE, jnp.float32),
        jnp.zeros((tok_slice, heads_dev), jnp.float32),
        jnp.zeros((tok_slice, heads_dev, LAT), jnp.float32),
    )
    piece_rows = lax.all_gather(prefix_latent, ("group", "tensor"), axis=0, tiled=True)
    prefix_spots = jnp.arange(piece_rows.shape[0], dtype=jnp.int32)
    page_hit = (prefix_spots // PAGE)[:, None] == jnp.arange(page_count, dtype=jnp.int32)[None, :]
    logical = (
        jnp.sum(jnp.where(page_hit, page_table[None, :], 0), axis=1) * PAGE + prefix_spots % PAGE
    )
    visible = (logical[None, :] >= range_low[:, None]) & (logical[None, :] < range_high[:, None])
    running = attend_block(start_state, query_rows, piece_rows, visible, heads_dev, score_scale)

    def suffix_step(running, key_rows, offset):
        key_spots = first_token - offset * tok_slice + jnp.arange(tok_slice, dtype=jnp.int32)
        visible = (key_spots[None, :] >= token_start[:, None]) & (
            key_spots[None, :] <= positions[:, None]
        )
        needed = token_start[0] <= key_spots[-1]

        def attend_here(state):
            return attend_block(state, query_rows, key_rows, visible, heads_dev, score_scale)

        def keep_state(state):
            return state

        return lax.cond(needed, attend_here, keep_state, running)

    running = suffix_step(running, suffix_latent, 0)
    for offset in range(1, REACH + 1):
        earlier = shifted(suffix_latent, "tensor", offset)
        running = suffix_step(running, earlier, offset)
    best_score, weight_sum, accumulated = running
    latent_out = (accumulated / weight_sum[:, :, None]).astype(jnp.bfloat16)
    head_out = (
        jnp.einsum("thl,hlv->thv", latent_out, value_up, preferred_element_type=jnp.float32)
        .astype(jnp.bfloat16)
        .reshape(tok_slice, -1)
    )
    attend_part = jnp.dot(head_out, output_weight, preferred_element_type=jnp.float32)
    gate_part = expert_gate[0]
    up_part = expert_up[0]
    down_part = expert_down[0]
    base_capacity = max(2, 4 * tok_quarter * top_count // (3 * expert_count))
    attend_full = lax.psum(attend_part.astype(jnp.bfloat16), "group").astype(jnp.float32)
    residual = (hidden_in.astype(jnp.float32) + attend_full).astype(jnp.bfloat16)
    normed = norm_rows(residual, norm_gain)
    route_ids = jnp.transpose(routes, (1, 0, 2)).reshape(tok_slice, top_count)
    weights = route_weights(normed, router, route_ids)
    capacity = groups * base_capacity
    targets = slot_targets(route_ids, expert_count, capacity)
    outgoing = pack_rows(normed, targets, expert_count * capacity).reshape(
        expert_count, capacity, width
    )
    partials = expert_apply(
        lax.all_to_all(outgoing, "tensor", split_axis=0, concat_axis=0, tiled=True),
        gate_part,
        up_part,
        down_part,
    )
    returned = lax.all_to_all(partials, "tensor", split_axis=0, concat_axis=0, tiled=True).reshape(
        expert_count * capacity, width
    )
    picked = jnp.take(returned, targets, axis=0)
    moe_part = jnp.sum(weights[:, :, None] * picked.astype(jnp.float32), axis=1)
    moe_share = lax.psum_scatter(
        moe_part.reshape(tok_quarter, groups, width).astype(jnp.bfloat16),
        "group",
        scatter_dimension=1,
        tiled=True,
    ).astype(jnp.float32)
    resid_quarter = lax.dynamic_slice_in_dim(
        residual.reshape(tok_quarter, groups, width), group_index, 1, 1
    )
    layer_rows = (resid_quarter.astype(jnp.float32) + moe_share).astype(jnp.bfloat16)
    normed_next = norm_rows(layer_rows, next_gain)
    query_cols = next_query_weight.shape[1]
    piece_rows = lax.all_gather(normed_next, "group", axis=1, tiled=True)
    query_part = jnp.einsum(
        "tmd,dc->tmc", piece_rows, next_query_weight, preferred_element_type=jnp.float32
    )
    latent_part = jnp.einsum(
        "tmd,dc->tmc", piece_rows, next_latent_weight, preferred_element_type=jnp.float32
    )
    projected = (
        jnp.concatenate([query_part, latent_part], axis=-1)
        .astype(jnp.bfloat16)
        .reshape(tok_slice, -1)
    )
    next_queries = projected[:, :query_cols]
    next_latent = projected[:, query_cols:]
    return (layer_rows, next_queries, next_latent)


def solution(mesh):
    return jax.shard_map(
        per_device,
        mesh=mesh,
        in_specs=(
            P("tensor", None),
            P("tensor", "group"),
            P("tensor", None),
            P(("group", "tensor"), None),
            P("group", None, None),
            P("group", None, None),
            P("group", None),
            P(),
            P(),
            P("tensor", None, "group"),
            P("tensor", None, "group"),
            P("tensor", "group", None),
            P(),
            P(None, "group"),
            P(None, "group"),
            P(),
            P(),
            P(),
            P(),
            P(None, "tensor", None),
        ),
        out_specs=(P("tensor", "group", None), P("tensor", "group"), P("tensor", "group")),
        check_vma=False,
    )
```

profile of v0, /device:TPU:1, one launch (start us, length us, event | category | flops | bytes accessed | tf_op | source)
XLA Modules:
  0.0 1171.9 jit_solution(3024611176863808069)
XLA Ops:
  9.8 10.3 collective-permute-start.3
  20.1 4.2 collective-permute-start.2
  26.3 3.0 collective-permute-start
  40.6 3.4 reduce-window.28
  51.9 2.2 reshape.485
  56.7 673.6 %all-gather.2.cloned.1.call-done = bf16[2048,576]{1,0:T(8,128)(2,1)} async-done(((bf16[8,576]{1,0:T(8,128)(2,1)}), bf16[2048,576]{1,0:T(8,128)(2,1)}) %all-gather.2.cloned.1.call-update) | async-done | bytes 2359312 | tf_op jit(solution)/shard_map/all_gather | solution.py:149
  730.3 4.1 fusion.28
  736.2 2.4 fusion.50
  738.6 20.6 %conditional.5 = (f32[128,4]{1,0:T(8,128)}, f32[128,4]{1,0:T(8,128)S(1)}, f32[128,4,512]{2,0,1:T(8,128)}) conditional(s32[]{:T(128)} %bitcast.20, (f32[128,4]{0,1:T(4,128)S(1)}, f32[128,4]{0,1:T(4,128)S(1)}, f32[128,4,512]{2,0,1:T(8,128)}) %tuple.46, (pred[128,128]{1,0:T(8,128)(4,1)}, bf16[512,576]{1,0:T(8,128)(2,1)}, bf16[128,576]{0,1:T(8,128)(2,1)}, ...), branch_computations={%region_9.10_spmd, %region_10.13_spmd} | conditional | flops 143590400 | bytes 4319284 | solution.py:171
  741.5 2.7 fusion.93
  748.6 2.3 fusion.1
  756.5 2.6 convolution_add_fusion
  768.5 99.8 %all-reduce.2.cloned.1.call-done = bf16[128,2048]{1,0:T(8,128)(2,1)} async-done(((bf16[128,2048]{1,0:T(8,128)(2,1)}), bf16[128,2048]{1,0:T(8,128)(2,1)}) %all-reduce.2.cloned.1.call-update) | async-done | bytes 524304 | tf_op jit(solution)/shard_map/psum | solution.py:189
  871.1 104.4 %all_to_all.10 = bf16[64,16,2048]{2,1,0:T(8,128)(2,1)S(1)} all-to-all(bf16[64,16,2048]{2,1,0:T(8,128)(2,1)S(1)} %bitcast.128), channel_id=1, replica_groups=mesh['group'=4,'tensor'=64] {'tensor'}, dimensions={0} | all-to-all | bytes 8388608 | tf_op jit(solution)/shard_map/all_to_all | solution.py:200
  977.5 2.9 fusion.45
  980.4 9.4 convolution_convert_fusion
  989.7 8.8 all-to-all-start.1
  1001.1 5.1 gather_fusion.1
  1007.0 82.8 %all-to-all-done.1 = bf16[64,16,2048]{2,1,0:T(8,128)(2,1)} async-done(((bf16[64,16,2048]{2,1,0:T(8,128)(2,1)}), bf16[64,16,2048]{2,1,0:T(8,128)(2,1)}, u32[]{:S(2)}, u32[]{:S(2)}) %all-to-all-start.1) | async-done | bytes 4194336 | tf_op jit(solution)/shard_map/all_to_all | solution.py:205
  1089.8 9.8 gather_fusion
  1099.6 6.3 reshape.501
  1105.9 6.8 multiply_reduce_fusion
  1120.3 31.3 %reduce-scatter.2.cloned.1.call-done = bf16[32,1,2048]{2,0,1:T(8,128)(2,1)} async-done(((bf16[32,4,2048]{2,0,1:T(8,128)(2,1)}), bf16[32,1,2048]{2,0,1:T(8,128)(2,1)}) %reduce-scatter.2.cloned.1.call-update) | async-done | bytes 131088 | tf_op jit(solution)/shard_map/reduce_scatter | solution.py:210
  1152.9 8.8 all_gather.7
  (153 shorter events, 67.0 us)
Async XLA Ops:
  7.2 1155.9 %copy-start = (bf16[2048,768]{1,0:T(8,128)(2,1)S(1)}, bf16[2048,768]{1,0:T(8,128)(2,1)}, u32[]{:S(2)}) copy-start(bf16[2048,768]{1,0:T(8,128)(2,1)} %param.43) | copy-start | bytes 9437188
  7.2 723.1 %all-gather.2.cloned.1.call-start = ((), (), s32[]{:S(2)}) async-start(), calls=%async_computation.3 | async-start | bytes 2631680 | tf_op jit(solution)/shard_map/all_gather | solution.py:149
  7.9 860.4 %all-reduce.2.cloned.1.call-start = ((), (), s32[]{:S(2)}) async-start(), calls=%async_computation.4 | async-start | bytes 1048576 | tf_op jit(solution)/shard_map/psum | solution.py:189
  9.8 752.1 %collective-permute-start.3 = (bf16[128,576]{1,0:T(8,128)(2,1)}, bf16[128,576]{1,0:T(8,128)(2,1)}, u32[]{:S(2)}, u32[]{:S(2)}) collective-permute-start(bf16[128,576]{1,0:T(8,128)(2,1)} %copy.185), channel_id=1, source_target_pairs={{0,4},{1,5},{2,6},{3,7},{4,8},{5,9},{6,10},{7,11},{8,12},{9,13},{1... | collective-permute-start | bytes 442376 | tf_op jit(solution)/shard_map/ppermute | solution.py:23
  20.1 739.1 %collective-permute-start.2 = (bf16[128,576]{1,0:T(8,128)(2,1)}, bf16[128,576]{1,0:T(8,128)(2,1)}, u32[]{:S(2)}, u32[]{:S(2)}) collective-permute-start(bf16[128,576]{1,0:T(8,128)(2,1)} %copy.185), channel_id=1, source_target_pairs={{0,3},{1,4},{2,5},{3,6},{4,7},{5,8},{6,9},{7,10},{8,11},{9,12},{10... | collective-permute-start | bytes 442376 | tf_op jit(solution)/shard_map/ppermute | solution.py:23
  24.3 734.8 %collective-permute-start.1 = (bf16[128,576]{1,0:T(8,128)(2,1)}, bf16[128,576]{1,0:T(8,128)(2,1)}, u32[]{:S(2)}, u32[]{:S(2)}) collective-permute-start(bf16[128,576]{1,0:T(8,128)(2,1)} %copy.185), channel_id=1, source_target_pairs={{0,2},{1,3},{2,4},{3,5},{4,6},{5,7},{6,8},{7,9},{8,10},{9,11},{10,... | collective-permute-start | bytes 442376 | tf_op jit(solution)/shard_map/ppermute | solution.py:23
  26.3 732.9 %collective-permute-start = (bf16[128,576]{1,0:T(8,128)(2,1)}, bf16[128,576]{1,0:T(8,128)(2,1)}, u32[]{:S(2)}, u32[]{:S(2)}) collective-permute-start(bf16[128,576]{1,0:T(8,128)(2,1)} %copy.185), channel_id=1, source_target_pairs={{0,1},{1,2},{2,3},{3,4},{4,5},{5,6},{6,7},{7,8},{8,9},{9,10},{10,1... | collective-permute-start | bytes 442376 | tf_op jit(solution)/shard_map/ppermute | solution.py:23
  29.3 25.7 %copy-start.13 = (s32[128]{0:T(128)}, s32[128]{0:T(128)S(1)}, u32[]{:S(2)}) copy-start(s32[128]{0:T(128)S(1)} %iota_add_fusion.4) | copy-start | bytes 1540
  29.9 2.4 copy-start.18
  32.3 21.8 %copy-start.23 = (s32[4]{0:T(128)S(1)}, s32[4]{0:T(128)}, u32[]{:S(2)}) copy-start(s32[4]{0:T(128)} %param.47) | copy-start | bytes 52
  33.1 21.1 %copy-start.17 = (s32[256]{0:T(256)S(1)}, s32[256]{0:T(256)}, u32[]{:S(2)}) copy-start(s32[256]{0:T(256)} %param.48) | copy-start | bytes 3076
  35.5 20.2 %copy-start.14 = (s32[128]{0:T(128)}, s32[128]{0:T(128)S(1)}, u32[]{:S(2)}) copy-start(s32[128]{0:T(128)S(1)} %get-tuple-element.255) | copy-start | bytes 1540
  730.3 4.2 copy-start.5
  759.2 2.7 copy-start.19
  762.0 2.1 copy-start.3
  762.0 3.8 copy-start.15
  762.0 3.8 copy-start.11
  869.8 105.7 %copy-start.1 = (bf16[128,2048]{1,0:T(8,128)(2,1)}, bf16[128,2048]{1,0:T(8,128)(2,1)S(1)}, u32[]{:S(2)}) copy-start(bf16[128,2048]{1,0:T(8,128)(2,1)S(1)} %get-tuple-element.273) | copy-start | bytes 1572868
  871.1 106.4 %copy-start.22 = (bf16[1,2048,352]{1,2,0:T(8,128)(2,1)S(1)}, bf16[1,2048,352]{1,2,0:T(8,128)(2,1)}, u32[]{:S(2)}) copy-start(bf16[1,2048,352]{1,2,0:T(8,128)(2,1)} %param.39) | copy-start | bytes 4325380
  989.7 8.9 copy-start.6
  989.7 100.1 %all-to-all-start.1 = ((bf16[64,16,2048]{2,1,0:T(8,128)(2,1)}), bf16[64,16,2048]{2,1,0:T(8,128)(2,1)}, u32[]{:S(2)}, u32[]{:S(2)}) async-start(bf16[64,16,2048]{2,1,0:T(8,128)(2,1)} %bitcast.129), calls=%async_computation.1 | async-start | bytes 8388608 | tf_op jit(solution)/shard_map/all_to_all | solution.py:205
  998.6 153.1 %reduce-scatter.2.cloned.1.call-start = ((), (), s32[]{:S(2)}) async-start(), calls=%async_computation.5 | async-start | bytes 655360 | tf_op jit(solution)/shard_map/reduce_scatter | solution.py:210
  1105.9 11.0 copy-start.16
  1152.7 10.9 copy-start.10
  (5 other events, 6.9 us)
Sparse Core Ops, SparseCore 0:
  9.9 720.3 all-gather.1
  765.5 102.7 all-reduce.1
  1117.0 34.5 reduce-scatter.1
where the time goes:
time: 1170 us
  waiting for transfers between devices  888 us (76%)
  blocking collectives  113 us (10%)
  local copies, waits for them, and re-layouts  63.8 us (5%)
  matrix products  33.6 us (3%)
  starting transfers between devices  28.4 us (2%)
  other arithmetic  26.9 us (2%)
  between operations  17.6 us (2%)
    all_gather x1, waiting for transfers between devices, per_device(): lax.all_gather(prefix_latent, ('group', 'tensor'), axis=0, tiled=True)  674 us
    all_to_all x1, blocking collectives, per_device(): lax.all_to_all(outgoing, 'tensor', split_axis=0, concat_axis=0, tiled=True)  104 us
    psum x1, waiting for transfers between devices, per_device(): lax.psum(attend_part.astype(jnp.bfloat16), 'group').astype(jnp.float32)  99.8 us
    all_to_all x1, waiting for transfers between devices, per_device(): lax.all_to_all(partials, 'tensor', split_axis=0, concat_axis=0, tiled=True)  82.8 us
    reduce_scatter x1, waiting for transfers between devices, per_device(): lax.psum_scatter(moe_part.reshape(tok_quarter, groups, width).astype(jnp....  31.3 us
  transfers between devices with their start and end apart: 8, of which 4 were waited for; matrix products, arithmetic and copies ran while one was open for 6% of the time, Pallas kernels for 0%

commit v1 on v0

v1 whole, which is shorter than its diff:
```python
import functools
import math

import jax
import jax.numpy as jnp
from jax import lax
from jax.experimental import pallas as pl
from jax.experimental.pallas import tpu as pltpu
from jax.sharding import PartitionSpec as P

NOPE = 128
ROPE = 64
LAT = 512
KEY = LAT + ROPE
PAGE = 8
REACH = 4
WIDTH = 2048
HALF = WIDTH // 2
EXPERTS = 64
TOP = 6
HEADS_DEV = 4
TOK = 128
QUARTER = 32
SLOTS = EXPERTS * 8
SCORE_SCALE = 1.0 / math.sqrt(NOPE + ROPE)
VERY_NEGATIVE = -1e30
ROUTE_SCALING = 2.446
NORM_EPSILON = 1e-06
BF16 = jnp.bfloat16
F32 = jnp.float32
MESH = pl.DeviceIdType.MESH
ANY = pl.BlockSpec(memory_space=pl.ANY)
VM = pl.BlockSpec(memory_space=pltpu.VMEM)
SM = pl.BlockSpec(memory_space=pltpu.SMEM)
DMA = pltpu.SemaphoreType.DMA
NT = (((1,), (1,)), ((), ()))
TN = (((0,), (0,)), ((), ()))


def coords():
    g = lax.axis_index("group")
    t = lax.axis_index("tensor")
    x = lax.div(g, 2) * 2 + lax.div(t, 32)
    y = lax.rem(lax.div(t, 8), 4)
    z = lax.rem(t, 8)
    return x, y, z, lax.rem(g, 2)


def group_of(x, c):
    return lax.div(x, 2) * 2 + c


def tensor_of(x, y, z):
    return (lax.rem(x, 2) * 4 + y) * 8 + z


def device(x, y, z, c):
    return {"group": group_of(x, c), "tensor": tensor_of(x, y, z)}


def remote(src, dst, send, recv, dev):
    return pltpu.make_async_remote_copy(
        src_ref=src, dst_ref=dst, send_sem=send, recv_sem=recv, device_id=dev, device_id_type=MESH
    )


def meet(peers):
    barrier = pltpu.get_barrier_semaphore()
    for peer in peers:
        pl.semaphore_signal(barrier, inc=1, device_id=peer, device_id_type=MESH)
    pl.semaphore_wait(barrier, len(peers))


def shape(dims, dtype=BF16):
    return jax.ShapeDtypeStruct(dims, dtype)


def params(cid=None, limit=56 << 20):
    if cid is None:
        return pltpu.CompilerParams(vmem_limit_bytes=limit)
    return pltpu.CompilerParams(collective_id=cid, has_side_effects=True, vmem_limit_bytes=limit)


def gather_kernel(pref, suf, pk, sk, own_sem, zs, zr, bs, br, cs, cr, us, ur, vs, vr, ws, wr):
    x, y, z, c = coords()
    g = lax.axis_index("group")
    t = lax.axis_index("tensor")
    sibling = device(x, y, z, 1 - c)
    opposite = device(lax.rem(x + 2, 4), y, z, c)
    z_dev = [None] + [device(x, y, lax.rem(z + d, 8), c) for d in range(1, 8)]
    p_dev = [None] + [
        device(lax.rem(x + d * c, 4), lax.rem(y + d * (1 - c), 4), z, c) for d in range(1, 4)
    ]
    q_dev = [None] + [
        device(lax.rem(x + d * (1 - c), 4), lax.rem(y + d * c, 4), z, c) for d in range(1, 4)
    ]
    ahead = [{"group": g, "tensor": lax.rem(t + k, 64)} for k in range(1, REACH + 1)]
    behind = [{"group": g, "tensor": lax.rem(t + 64 - k, 64)} for k in range(1, REACH + 1)]
    meet(z_dev[1:] + p_dev[1:] + q_dev[1:] + [sibling] + ahead + behind)

    def block(dp, dq, core):
        bx = lax.rem(x + 8 - dp * core - dq * (1 - core), 4)
        by = lax.rem(y + 8 - dp * (1 - core) - dq * core, 4)
        return pk.at[pl.ds(group_of(bx, core) * 64 + tensor_of(bx, by, 0), 8)]

    sends = []

    def go(src, dst, send, recv, dev):
        copy = remote(src, dst, send, recv, dev)
        copy.start()
        sends.append(copy)

    me = g * 64 + t
    own = pltpu.make_async_copy(pref, pk.at[me], own_sem)
    own.start()
    for d in range(1, 8):
        go(pref, pk.at[me], zs.at[d], zr.at[d], z_dev[d])
    for k in range(REACH):
        go(suf.at[g], sk.at[k, g], us.at[k], ur.at[k], ahead[k])
    own.wait()
    base = me - z
    for d in range(1, 8):
        row = pk.at[base + lax.rem(z + 8 - d, 8)]
        remote(pref, row, zs.at[d], zr.at[d], z_dev[d]).wait_recv()
    first = block(0, 0, c)
    for d in range(1, 4):
        go(first, first, bs.at[d, 0], br.at[d, 0], p_dev[d])
    for d in range(1, 4):
        go(first, first, bs.at[0, d], br.at[0, d], q_dev[d])
    go(first, first, cs.at[0, 0], cr.at[0, 0], sibling)
    for dp in range(1, 4):
        here = block(dp, 0, c)
        remote(here, here, bs.at[dp, 0], br.at[dp, 0], sibling).wait_recv()
        for d in range(1, 4):
            go(here, here, bs.at[dp, d], br.at[dp, d], q_dev[d])
        go(here, here, cs.at[dp, 0], cr.at[dp, 0], sibling)
    for k in range(REACH):
        here = sk.at[k, g]
        remote(here, here, us.at[k], ur.at[k], sibling).wait_recv()
        go(here, here, vs.at[k], vr.at[k], opposite)
        go(here, here, ws.at[k, 0], wr.at[k, 0], sibling)
    for dp in range(4):
        for dq in range(1, 4):
            here = block(dp, dq, c)
            remote(here, here, bs.at[dp, dq], br.at[dp, dq], sibling).wait_recv()
            go(here, here, cs.at[dp, dq], cr.at[dp, dq], sibling)
    far = lax.rem(g + 2, 4)
    for k in range(REACH):
        here = sk.at[k, far]
        remote(here, here, vs.at[k], vr.at[k], sibling).wait_recv()
        go(here, here, ws.at[k, 1], wr.at[k, 1], sibling)
    for dp in range(4):
        for dq in range(4):
            here = block(dp, dq, 1 - c)
            remote(here, here, cs.at[dp, dq], cr.at[dp, dq], sibling).wait_recv()
    near = g + 1 - 2 * c
    for k in range(REACH):
        for side, who in ((0, near), (1, lax.rem(near + 2, 4))):
            here = sk.at[k, who]
            remote(here, here, ws.at[k, side], wr.at[k, side], sibling).wait_recv()
    for copy in sends:
        copy.wait_send()


def gather_keys(prefix_rows, suffix_rows):
    sems = [DMA(()), DMA((8,)), DMA((8,)), DMA((4, 4)), DMA((4, 4)), DMA((4, 4)), DMA((4, 4))]
    sems += [DMA((REACH,))] * 4 + [DMA((REACH, 2))] * 2
    return pl.pallas_call(
        gather_kernel,
        out_shape=(shape((256, PAGE, KEY)), shape((REACH, 4, QUARTER, KEY))),
        in_specs=[ANY, ANY],
        out_specs=(ANY, ANY),
        scratch_shapes=sems,
        compiler_params=params(0),
        name="gather_keys",
    )(prefix_rows, suffix_rows)


def slot_kernel(routes, member, select):
    rows = 2 * QUARTER
    experts = lax.broadcasted_iota(jnp.int32, (rows, EXPERTS), 1)
    hit = jnp.zeros((rows, EXPERTS), F32)
    for k in range(TOP):
        hit = hit + (routes[:, k : k + 1] == experts).astype(F32)
    member[...] = hit
    i = lax.broadcasted_iota(jnp.int32, (rows, rows), 0)
    j = lax.broadcasted_iota(jnp.int32, (rows, rows), 1)
    before = ((j < i) & ((j >> 5) == (i >> 5))).astype(BF16)
    hits = hit.astype(BF16)
    rank = jnp.dot(before, hits, preferred_element_type=F32)
    spread = spread_matrix()
    hit_wide = jnp.dot(hits, spread, preferred_element_type=F32)
    rank_wide = jnp.dot(rank.astype(BF16), spread, preferred_element_type=F32)
    col = lax.broadcasted_iota(jnp.int32, (rows, SLOTS), 1)
    row = lax.broadcasted_iota(jnp.int32, (rows, SLOTS), 0)
    slot = (col & 3).astype(F32)
    chosen = (hit_wide > 0.5) & (rank_wide == slot) & (((col >> 2) & 1) == (row >> 5))
    select[...] = chosen.astype(BF16)


def spread_matrix():
    e = lax.broadcasted_iota(jnp.int32, (EXPERTS, SLOTS), 0)
    col = lax.broadcasted_iota(jnp.int32, (EXPERTS, SLOTS), 1)
    owner = ((col >> 3) & 1) * 32 + (col >> 4)
    return (e == owner).astype(BF16)


def slots(routes_chip):
    return pl.pallas_call(
        slot_kernel,
        out_shape=(shape((64, EXPERTS), F32), shape((64, SLOTS))),
        in_specs=[VM],
        out_specs=(VM, VM),
        compiler_params=params(),
        name="slots",
    )(routes_chip)


def attend_kernel(first_s, lens, tenants, spans, pages, q, ku, vu, ow, pk, sk, own, out, bias, s, acc):
    first = first_s[0]
    r = lax.broadcasted_iota(jnp.int32, (TOK, 1), 0)
    pos = first + (r & 31) * 4 + (r >> 5)

    def one_request(i, state):
        start, begin, low, high = state
        end = start + lens[i]
        inside = (pos >= start) & (pos < end)
        tenant = tenants[i]
        lo = jnp.int32(0)
        for k in range(3):
            lo = lo + jnp.where(k < tenant, spans[k], 0)
        hi = lo + spans[tenant]
        begin = jnp.where(inside, start, begin)
        low = jnp.where(inside, lo, low)
        high = jnp.where(inside, hi, high)
        return end, begin, low, high

    zero = jnp.zeros((TOK, 1), jnp.int32)
    _, begin, low, high = lax.fori_loop(0, 32, one_request, (jnp.int32(0), zero, zero, zero))
    page = lax.broadcasted_iota(jnp.int32, (256, 2048), 0)
    spot = lax.broadcasted_iota(jnp.int32, (256, 2048), 1)
    expand = (page == (spot >> 3)).astype(BF16)
    table = jnp.broadcast_to(pages[...], (8, 256)).astype(F32).astype(BF16)
    logical = jnp.dot(table, expand, preferred_element_type=F32)[0:1].astype(jnp.int32) * PAGE
    logical = logical + (lax.broadcasted_iota(jnp.int32, (1, 2048), 1) & 7)
    seen = (logical >= low) & (logical < high)
    bias[:, 0:2048] = jnp.where(seen, 0.0, VERY_NEGATIVE)
    col = lax.broadcasted_iota(jnp.int32, (1, 640), 1)
    step = col >> 7
    spot = first + (col & 127) - jnp.where(step == 4, 0, (step + 1) * TOK)
    seen = (spot >= begin) & (spot <= pos)
    bias[:, 2048:2688] = jnp.where(seen, 0.0, VERY_NEGATIVE)
    acc[...] = jnp.zeros_like(acc)

    def one_head(h, _):
        qh = q[h]
        absorbed = jnp.dot(qh[:, :NOPE], ku[h], preferred_element_type=F32).astype(BF16)
        full = jnp.concatenate([absorbed, qh[:, NOPE:]], axis=1)
        pieces = ((pk, 0, 2048), (sk, 2048, 2560), (own, 2560, 2688))
        for keys, lo, hi in pieces:
            scores = lax.dot_general(full, keys[...], NT, preferred_element_type=F32)
            s[:, lo:hi] = scores * SCORE_SCALE + bias[:, lo:hi]
        best = jnp.max(s[...], axis=1, keepdims=True)
        total = jnp.zeros((TOK, 1), F32)
        mixed = jnp.zeros((TOK, LAT), F32)
        for keys, lo, hi in pieces:
            weights = jnp.exp(s[:, lo:hi] - best)
            total = total + jnp.sum(weights, axis=1, keepdims=True)
            mixed = mixed + jnp.dot(
                weights.astype(BF16), keys[:, :LAT], preferred_element_type=F32
            )
        latent = (mixed / total).astype(BF16)
        head = jnp.dot(latent, vu[h], preferred_element_type=F32).astype(BF16)
        acc[...] += jnp.dot(head, ow[h], preferred_element_type=F32)
        return 0

    lax.fori_loop(0, HEADS_DEV, one_head, 0)
    out[...] = acc[...].astype(BF16)


def attend(first, lens, tenants, spans, pages, q, ku, vu, ow, pk, sk, own):
    return pl.pallas_call(
        attend_kernel,
        out_shape=shape((TOK, WIDTH)),
        in_specs=[SM, SM, SM, SM] + [VM] * 8,
        out_specs=VM,
        scratch_shapes=[
            pltpu.VMEM((TOK, 2688), F32),
            pltpu.VMEM((TOK, 2688), F32),
            pltpu.VMEM((TOK, WIDTH), F32),
        ],
        compiler_params=params(),
        name="attend",
    )(first, lens, tenants, spans, pages, q, ku, vu, ow, pk, sk, own)


def normalized(values, gain):
    mean_square = jnp.sum(values * values, axis=-1, keepdims=True) * (1.0 / WIDTH)
    return (values * lax.rsqrt(mean_square + NORM_EPSILON) * gain.astype(F32)).astype(BF16)


def reduce_kernel(att, hq, gain, select, packed, resid, rows, near, half, far, both, ns, nr, fs, fr, ts, tr):
    x, y, z, c = coords()
    xh = lax.div(x, 2)
    sibling = device(x, y, z, 1 - c)
    opposite = device(lax.rem(x + 2, 4), y, z, c)
    meet([sibling, opposite])
    to_near = []
    for k in range(2):
        copy = remote(att.at[2 * k + 1 - c], near.at[k], ns.at[k], nr.at[k], sibling)
        copy.start()
        to_near.append(copy)
    for copy in to_near:
        copy.wait()
    half[...] = (att[2 * (1 - xh) + c].astype(F32) + near[1 - xh].astype(F32)).astype(BF16)
    across = remote(half, far, fs, fr, opposite)
    across.start()
    mine = att[2 * xh + c].astype(F32) + near[xh].astype(F32) + hq[...].astype(F32)
    across.wait()
    residual = (mine + far[...].astype(F32)).astype(BF16)
    resid[...] = residual
    both[c] = normalized(residual.astype(F32), gain[...])
    share = remote(both.at[c], both.at[c], ts, tr, sibling)
    share.start()
    share.wait_send()
    remote(both.at[1 - c], both.at[1 - c], ts, tr, sibling).wait_recv()
    rows[...] = both[...].reshape(64, WIDTH)
    part = both[:, :, pl.ds(pl.multiple_of(c * HALF, HALF), HALF)].reshape(64, HALF)
    out = lax.dot_general(select[...], part, TN, preferred_element_type=F32).astype(BF16)
    packed[...] = out.reshape(32, 2, 8, HALF)


def reduce_group(att, hq, gain, select):
    return pl.pallas_call(
        reduce_kernel,
        out_shape=(shape((32, 2, 8, HALF)), shape((QUARTER, WIDTH)), shape((64, WIDTH))),
        in_specs=[VM] * 4,
        out_specs=(VM, VM, VM),
        scratch_shapes=[
            pltpu.VMEM((2, QUARTER, WIDTH), BF16),
            pltpu.VMEM((QUARTER, WIDTH), BF16),
            pltpu.VMEM((QUARTER, WIDTH), BF16),
            pltpu.VMEM((2, QUARTER, WIDTH), BF16),
            DMA((2,)),
            DMA((2,)),
            DMA(()),
            DMA(()),
            DMA(()),
            DMA(()),
        ],
        compiler_params=params(1),
        name="reduce_group",
    )(att, hq, gain, select)


LAG = 4


def dispatch_kernel(packed, rows, land, s1, r1, ls, xs, xr, cs, cr):
    x, y, z, c = coords()
    xl = lax.rem(x, 2)
    here = y * 8 + z
    sibling = device(x, y, z, 1 - c)
    x_dev = [None] + [device(lax.rem(x + d, 4), y, z, c) for d in range(1, 4)]
    barrier = pltpu.get_barrier_semaphore()

    def yz_dev(s):
        return device(x, lax.rem(y + lax.div(s, 8), 4), lax.rem(z + lax.rem(s, 8), 8), c)

    def yz_to(s):
        return lax.rem(y + lax.div(s, 8), 4) * 8 + lax.rem(z + lax.rem(s, 8), 8)

    def yz_from(s):
        return lax.rem(y + 4 - lax.div(s, 8), 4) * 8 + lax.rem(z + 8 - lax.rem(s, 8), 8)

    def greet(s, _):
        pl.semaphore_signal(barrier, inc=1, device_id=yz_dev(s), device_id_type=MESH)
        return 0

    lax.fori_loop(1, 32, greet, 0)
    for peer in x_dev[1:] + [sibling]:
        pl.semaphore_signal(barrier, inc=1, device_id=peer, device_id_type=MESH)
    pl.semaphore_wait(barrier, 35)

    def first_leg(s):
        return remote(packed.at[yz_to(s)], land.at[here], s1.at[s], r1.at[s], yz_dev(s))

    def x_leg(s, d, src):
        spot = rows.at[c, x, yz_from(s)]
        return remote(src, spot, xs.at[d, s], xr.at[d, s], x_dev[d])

    def to_sibling(s, d, src):
        spot = rows.at[c, lax.rem(x + d, 4), yz_from(s)]
        return remote(src, spot, cs.at[d, s], cr, sibling)

    def local(s, src):
        return pltpu.make_async_copy(src, rows.at[c, x, yz_from(s)], ls.at[s])

    def start_first(s, _):
        first_leg(s).start()
        return 0

    lax.fori_loop(1, 32, start_first, 0)
    keep = pltpu.make_async_copy(packed.at[here], land.at[here], s1.at[0])
    keep.start()
    keep.wait()

    def forward(s):
        block = yz_from(s)
        same, other = land.at[block, xl], land.at[block, 1 - xl]
        x_leg(s, 2, same).start()
        x_leg(s, 1, other).start()
        x_leg(s, 3, other).start()
        to_sibling(s, 0, same).start()
        local(s, same).start()

    def pass_on(s):
        for d in (1, 3, 2):
            spot = rows.at[c, lax.rem(x + d, 4), yz_from(s)]
            remote(spot, spot, xs.at[4 - d, s], xr.at[4 - d, s], sibling).wait_recv()
            to_sibling(s, d, spot).start()

    forward(0)

    def step(s, _):
        spot = land.at[yz_from(s)]
        remote(spot, spot, s1.at[s], r1.at[s], sibling).wait_recv()
        forward(s)

        @pl.when(s >= LAG)
        def _():
            pass_on(s - LAG)

        return 0

    lax.fori_loop(1, 32, step, 0)

    def rest(s, _):
        pass_on(s)
        return 0

    lax.fori_loop(32 - LAG, 32, rest, 0)
    remote(rows.at[1 - c], rows.at[1 - c], cs.at[0, 0], cr, sibling).wait_recv()

    def drain(s, _):
        block = yz_from(s)
        same = land.at[block, 0]
        for d in range(1, 4):
            x_leg(s, d, same).wait_send()
        for d in range(4):
            to_sibling(s, d, same).wait_send()
        local(s, same).wait()

        @pl.when(s >= 1)
        def _():
            first_leg(s).wait_send()

        return 0

    lax.fori_loop(0, 32, drain, 0)


def dispatch(packed):
    return pl.pallas_call(
        dispatch_kernel,
        out_shape=shape((2, 4, 32, 8, HALF)),
        in_specs=[ANY],
        out_specs=ANY,
        scratch_shapes=[
            pltpu.VMEM((32, 2, 8, HALF), BF16),
            DMA((32,)),
            DMA((32,)),
            DMA((32,)),
            DMA((4, 32)),
            DMA((4, 32)),
            DMA((4, 32)),
            DMA(()),
        ],
        compiler_params=params(2),
        name="dispatch",
    )(packed)


def split_terms(values, count):
    terms = []
    for _ in range(count):
        term = values.astype(BF16)
        terms.append(term)
        values = values - term.astype(F32)
    return terms


def expert_kernel(rows, gate, up, down, normed, router, member, select, out, mix):
    @pl.when(pl.program_id(0) == 0)
    def _():
        logits = jnp.dot(normed[...], router[...], preferred_element_type=F32)
        picked = jax.nn.sigmoid(logits) * member[...]
        weights = picked / jnp.sum(picked, axis=1, keepdims=True) * ROUTE_SCALING
        spread = spread_matrix()
        wide = jnp.zeros((64, SLOTS), F32)
        for term in split_terms(weights, 3):
            wide = wide + jnp.dot(term, spread, preferred_element_type=F32)
        wide = wide * select[...].astype(F32)
        for k, term in enumerate(split_terms(wide, 2)):
            mix[k] = term

    left, right = rows[0], rows[1]

    def product(weight):
        return jnp.dot(left, weight[:HALF], preferred_element_type=F32) + jnp.dot(
            right, weight[HALF:], preferred_element_type=F32
        )

    gate_vals = product(gate)
    hidden = (gate_vals / (1.0 + jnp.exp(-gate_vals)) * product(up)).astype(BF16)
    result = jnp.dot(hidden, down[...], preferred_element_type=F32).astype(BF16)
    out[0] = result[:, :HALF]
    out[1] = result[:, HALF:]


def experts(rows, gate, up, down, normed, router, member, select):
    chunk = 128
    whole = lambda *dims: pl.BlockSpec(dims, lambda i: (0,) * len(dims))
    moving = pl.BlockSpec((2, chunk, HALF), lambda i: (0, i, 0))
    ff = gate.shape[1]
    return pl.pallas_call(
        expert_kernel,
        out_shape=(shape((2, 1024, HALF)), shape((2, 64, SLOTS))),
        grid=(1024 // chunk,),
        in_specs=[
            moving,
            whole(WIDTH, ff),
            whole(WIDTH, ff),
            whole(ff, WIDTH),
            whole(64, WIDTH),
            whole(WIDTH, EXPERTS),
            whole(64, EXPERTS),
            whole(64, SLOTS),
        ],
        out_specs=(moving, whole(2, 64, SLOTS)),
        compiler_params=params(),
        name="experts",
    )(rows, gate, up, down, normed, router, member, select)


def combine_kernel(
    parts, mix, resid, gain, wq, wl, layer, nq, nl,
    near, summed, landed, turned, back, moe, other, normed,
    ns, nr, xs, xr, bs, br, es, er, hs, hr,
):
    x, y, z, c = coords()
    g = lax.axis_index("group")
    xl = lax.rem(x, 2)
    here = y * 8 + z
    sibling = device(x, y, z, 1 - c)
    x_dev = [None] + [device(lax.rem(x + d, 4), y, z, c) for d in range(1, 4)]
    barrier = pltpu.get_barrier_semaphore()

    def yz_dev(s):
        return device(x, lax.rem(y + lax.div(s, 8), 4), lax.rem(z + lax.rem(s, 8), 8), c)

    def yz_to(s):
        return lax.rem(y + lax.div(s, 8), 4) * 8 + lax.rem(z + lax.rem(s, 8), 8)

    def yz_from(s):
        return lax.rem(y + 4 - lax.div(s, 8), 4) * 8 + lax.rem(z + 8 - lax.rem(s, 8), 8)

    def greet(s, _):
        pl.semaphore_signal(barrier, inc=1, device_id=yz_dev(s), device_id_type=MESH)
        return 0

    lax.fori_loop(1, 32, greet, 0)
    for peer in x_dev[1:] + [sibling]:
        pl.semaphore_signal(barrier, inc=1, device_id=peer, device_id_type=MESH)
    pl.semaphore_wait(barrier, 35)

    def span(j):
        return pl.ds(pl.multiple_of(lax.rem(y + j, 4) * 8, 8), 8)

    order = (2, 1, 3, 0)

    def near_copy(j, d):
        xd = lax.rem(x + d, 4)
        return remote(
            parts.at[1 - c, xd, span(j)], near.at[xd, span(j)], ns.at[j, d], nr.at[j, d], sibling
        )

    def x_copy(j, d):
        xd = lax.rem(x + d, 4)
        return remote(
            summed.at[xd, span(j)], landed.at[d, span(j)], xs.at[j, d], xr.at[j, d], x_dev[d]
        )

    def back_copy(s):
        return remote(turned.at[yz_to(s)], back.at[here], bs.at[s], br.at[s], yz_dev(s))

    def start_near(j, _):
        for d in order:
            near_copy(j, d).start()
        return 0

    lax.fori_loop(0, 4, start_near, 0)

    def sum_near(j, _):
        for d in order:
            near_copy(j, d).wait_recv()
            xd = lax.rem(x + d, 4)
            total = parts[c, xd, span(j)].astype(F32) + near[xd, span(j)].astype(F32)
            summed[xd, span(j)] = total.astype(BF16)
            if d > 0:
                x_copy(j, d).start()
        return 0

    lax.fori_loop(0, 4, sum_near, 0)

    def sum_x(j, _):
        for d in range(1, 4):
            x_copy(j, d).wait_recv()
        same = summed[x, span(j)].astype(F32) + landed[2, span(j)].astype(F32)
        cross = landed[1, span(j)].astype(F32) + landed[3, span(j)].astype(F32)
        turned[span(j), xl] = same.astype(BF16)
        turned[span(j), 1 - xl] = cross.astype(BF16)
        for k in range(8):
            s = j * 8 + k

            @pl.when(s >= 1)
            def _():
                back_copy(s).start()

        return 0

    lax.fori_loop(0, 4, sum_x, 0)
    back[here] = turned[here]

    def arrive(s, _):
        spot = back.at[yz_from(s)]
        remote(spot, spot, bs.at[s], br.at[s], sibling).wait_recv()
        return 0

    lax.fori_loop(1, 32, arrive, 0)
    values = back[...].reshape(SLOTS, HALF)
    gated = jnp.dot(mix[0], values, preferred_element_type=F32)
    gated = gated + jnp.dot(mix[1], values, preferred_element_type=F32)
    moe[...] = gated.reshape(2, QUARTER, HALF)
    swap = remote(moe.at[1 - c], other, es, er, sibling)
    swap.start()
    mine = pl.ds(pl.multiple_of(c * HALF, HALF), HALF)
    theirs = pl.ds(pl.multiple_of((1 - c) * HALF, HALF), HALF)
    layer[:, mine] = (resid[:, mine].astype(F32) + moe[c]).astype(BF16)
    swap.wait()
    layer[:, theirs] = (resid[:, theirs].astype(F32) + other[...]).astype(BF16)
    normed[g] = normalized(layer[...].astype(F32), gain[...])
    gs = g + 1 - 2 * c
    far, far_s = lax.rem(g + 2, 4), lax.rem(gs + 2, 4)

    def share(k, who, dev):
        return remote(normed.at[who], normed.at[who], hs.at[k], hr.at[k], dev)

    def project(who):
        block = normed[who]
        nq[who] = jnp.dot(block, wq[...], preferred_element_type=F32).astype(BF16)
        nl[who] = jnp.dot(block, wl[...], preferred_element_type=F32).astype(BF16)

    share(0, g, x_dev[2]).start()
    share(1, g, sibling).start()
    project(g)
    share(1, gs, sibling).wait_recv()
    project(gs)
    share(0, far, sibling).wait_recv()
    share(2, far, sibling).start()
    project(far)
    share(2, far_s, sibling).wait_recv()
    project(far_s)
    share(0, g, x_dev[2]).wait_send()
    share(1, g, sibling).wait_send()
    share(2, far, sibling).wait_send()

    def drain(j, _):
        for d in order:
            near_copy(j, d).wait_send()
            if d > 0:
                x_copy(j, d).wait_send()
        for k in range(8):
            s = j * 8 + k

            @pl.when(s >= 1)
            def _():
                back_copy(s).wait_send()

        return 0

    lax.fori_loop(0, 4, drain, 0)


def combine(parts, mix, resid, gain, wq, wl):
    cols, lat = wq.shape[1], wl.shape[1]
    return pl.pallas_call(
        combine_kernel,
        out_shape=(
            shape((QUARTER, WIDTH)),
            shape((4, QUARTER, cols)),
            shape((4, QUARTER, lat)),
        ),
        in_specs=[VM] * 6,
        out_specs=(VM, VM, VM),
        scratch_shapes=[
            pltpu.VMEM((4, 32, 8, HALF), BF16),
            pltpu.VMEM((4, 32, 8, HALF), BF16),
            pltpu.VMEM((4, 32, 8, HALF), BF16),
            pltpu.VMEM((32, 2, 8, HALF), BF16),
            pltpu.VMEM((32, 2, 8, HALF), BF16),
            pltpu.VMEM((2, QUARTER, HALF), F32),
            pltpu.VMEM((QUARTER, HALF), F32),
            pltpu.VMEM((4, QUARTER, WIDTH), BF16),
            DMA((4, 4)),
            DMA((4, 4)),
            DMA((4, 4)),
            DMA((4, 4)),
            DMA((32,)),
            DMA((32,)),
            DMA(()),
            DMA(()),
            DMA((3,)),
            DMA((3,)),
        ],
        compiler_params=params(3),
        name="combine",
    )(parts, mix, resid, gain, wq, wl)


def per_device(
    hidden_in,
    queries,
    suffix_latent,
    prefix_latent,
    key_up,
    value_up,
    output_weight,
    norm_gain,
    router,
    expert_gate,
    expert_up,
    expert_down,
    next_gain,
    next_query_weight,
    next_latent_weight,
    suffix_lengths,
    request_tenant,
    tenant_lengths,
    page_table,
    routes,
):
    g = lax.axis_index("group")
    first = (lax.axis_index("tensor") * TOK).astype(jnp.int32).reshape(1)
    pk, sk = gather_keys(prefix_latent, suffix_latent.reshape(4, QUARTER, KEY))
    q = queries.reshape(QUARTER, 4, HEADS_DEV, NOPE + ROPE).transpose(2, 1, 0, 3)
    att = attend(
        first,
        suffix_lengths,
        request_tenant,
        tenant_lengths,
        page_table.reshape(1, -1),
        q.reshape(HEADS_DEV, TOK, NOPE + ROPE),
        key_up,
        value_up,
        output_weight.reshape(HEADS_DEV, NOPE, WIDTH),
        pk.reshape(-1, KEY),
        sk.reshape(-1, KEY),
        suffix_latent,
    )
    chip_routes = lax.dynamic_slice_in_dim(routes, (g // 2) * 2, 2, 0).reshape(64, TOP)
    member, select = slots(chip_routes)
    hq = lax.dynamic_slice_in_dim(hidden_in.reshape(QUARTER, 4, WIDTH), g, 1, 1)
    packed, resid, normed = reduce_group(
        att.reshape(4, QUARTER, WIDTH), hq.reshape(QUARTER, WIDTH), norm_gain.reshape(1, -1), select
    )
    rows = dispatch(packed)
    parts, mix = experts(
        rows.reshape(2, 1024, HALF),
        expert_gate[0],
        expert_up[0],
        expert_down[0],
        normed,
        router,
        member,
        select,
    )
    layer, nq, nl = combine(
        parts.reshape(2, 4, 32, 8, HALF),
        mix,
        resid,
        next_gain.reshape(1, -1),
        next_query_weight,
        next_latent_weight,
    )
    nq = nq.transpose(1, 0, 2).reshape(TOK, -1)
    nl = nl.transpose(1, 0, 2).reshape(TOK, -1)
    return layer.reshape(QUARTER, 1, WIDTH), nq, nl


def solution(mesh):
    return jax.shard_map(
        per_device,
        mesh=mesh,
        in_specs=(
            P("tensor", None),
            P("tensor", "group"),
            P("tensor", None),
            P(("group", "tensor"), None),
            P("group", None, None),
            P("group", None, None),
            P("group", None),
            P(),
            P(),
            P("tensor", None, "group"),
            P("tensor", None, "group"),
            P("tensor", "group", None),
            P(),
            P(None, "group"),
            P(None, "group"),
            P(),
            P(),
            P(),
            P(),
            P(None, "tensor", None),
        ),
        out_specs=(P("tensor", "group", None), P("tensor", "group"), P("tensor", "group")),
        check_vma=False,
    )
```

time: 1170 us -> 199 us (0.17)
  waiting for transfers between devices: 888 us -> 0 us
  Pallas kernels: 0 us -> 180 us
  blocking collectives: 113 us -> 0 us
  local copies, waits for them, and re-layouts: 63.8 us -> 17.2 us
  matrix products: 33.6 us -> 0 us
  starting transfers between devices: 28.4 us -> 0 us
  other arithmetic: 26.9 us -> 0 us
  between operations: 17.6 us -> 0.79 us
    all_gather x1 -> x0, waiting for transfers between devices: 674 us -> none  [per_device(): lax.all_gather(prefix_latent, ('group', 'tensor'), axis=0, tiled=True)]
    pallas_call x0 -> x7, Pallas kernels: none -> 180 us  [the longest x1 54.1 us: combine(): pl.pallas_call(combine_kernel, out_shape=(shape((QUARTER, WIDTH)), shape(...]
    all_to_all x1 -> x0, blocking collectives: 104 us -> none  [per_device(): lax.all_to_all(outgoing, 'tensor', split_axis=0, concat_axis=0, tiled=True)]
    psum x1 -> x0, waiting for transfers between devices: 99.8 us -> none  [per_device(): lax.psum(attend_part.astype(jnp.bfloat16), 'group').astype(jnp.float32)]
    all_to_all x1 -> x0, waiting for transfers between devices: 82.8 us -> none  [per_device(): lax.all_to_all(partials, 'tensor', split_axis=0, concat_axis=0, tiled=True)]
    dot_general x13 -> x0, matrix products: 33.6 us -> none  [the longest x1 9.36 us: expert_apply(): jnp.dot(hidden_vals, down_part, preferred_element_type=jnp.float32)]
    reduce_scatter x1 -> x0, waiting for transfers between devices: 31.3 us -> none  [per_device(): lax.psum_scatter(moe_part.reshape(tok_quarter, groups, width).astype(jnp....]
    gather x8 -> x0, local copies, waits for them, and re-layouts: 21.8 us -> none  [the longest x2 16.1 us: per_device(): picked = jnp.take(returned, targets, axis=0)]
  transfers between devices with their start and end apart: 8 -> 0, of which waited for: 4 -> 0; matrix products, arithmetic and copies ran while one was open for 6% -> 0% of each run, Pallas kernels for 0% -> 0%
where the time goes in v1:
time: 199 us; the launch traced here: 198 us
  Pallas kernels  180 us (90%)
  local copies, waits for them, and re-layouts  17.2 us (9%)
    pallas_call x1, Pallas kernels, combine(): pl.pallas_call(combine_kernel, out_shape=(shape((QUARTER, WIDTH)), shape(...  54.1 us
    pallas_call x1, Pallas kernels, dispatch(): pl.pallas_call(dispatch_kernel, out_shape=shape((2, 4, 32, 8, HALF)), in_...  45.5 us
    pallas_call x1, Pallas kernels, gather_keys(): pl.pallas_call(gather_kernel, out_shape=(shape((256, PAGE, KEY)), shape((...  38.2 us
    pallas_call x1, Pallas kernels, attend(): pl.pallas_call(attend_kernel, out_shape=shape((TOK, WIDTH)), in_specs=[SM...  14.9 us
    pallas_call x1, Pallas kernels, experts(): pl.pallas_call(expert_kernel, out_shape=(shape((2, 1024, HALF)), shape((2...  13.4 us
    pallas_call x1, Pallas kernels, reduce_group(): pl.pallas_call(reduce_kernel, out_shape=(shape((32, 2, 8, HALF)), shape((...  12.5 us
    unnamed x26, local copies, waits for them, and re-layouts  10 us

profile of v1, /device:TPU:1, one launch (start us, length us, event | category | flops | bytes accessed | tf_op | source)
XLA Modules:
  0.0 198.4 jit_solution(1502958526123701640)
XLA Ops:
  0.7 0.7 copy-done
  1.4 0.7 copy.36
  2.1 1.8 slots.1
  3.9 1.2 reshape.72
  5.4 0.7 copy.46
  6.1 0.8 copy.33.own
  6.9 38.2 %gather_keys.1 = (bf16[256,8,576]{2,1,0:T(8,128)(2,1)}, bf16[4,4,32,576]{3,2,1,0:T(8,128)(2,1)}) custom-call(bf16[8,576]{1,0:T(8,128)(2,1)} %pref.1, bf16[4,32,576]{2,1,0:T(8,128)(2,1)} %bitcast.29), custom_call_target="tpu_custom_call" | custom-call | tf_op jit(solution)/shard_map/gather_keys/pallas_call | solution.py:168
  45.5 0.8 copy.32
  46.2 14.9 %attend.1 = bf16[128,2048]{1,0:T(8,128)(2,1)} custom-call(s32[1]{0:T(128)} %bitcast.first_s, s32[32]{0:T(128)} %lens.1, s32[32]{0:T(128)} %tenants.1, s32[4]{0:T(128)} %spans.1, s32[1,256]{1,0:T(1,128)} %bitcast.38, bf16[4,128,192]{2,1,0:T(8,128)(2,1)} %bitcast.31, bf16[4,128,512]{2,1,0:T(8,128)(2,1)} %ku.1, bf16[4,512,128]{2,1,0:T(8,128)(2,1)} %vu.1, ...), custom_call_target="tpu_custom_call" | custom-call | tf_op jit(solution)/shard_map/attend/pallas_call | solution.py:282
  61.1 0.6 reshape.74.gain
  61.7 12.5 %reduce_group.1 = (bf16[32,2,8,1024]{3,2,1,0:T(8,128)(2,1)}, bf16[32,2048]{1,0:T(8,128)(2,1)}, bf16[64,2048]{1,0:T(8,128)(2,1)}) custom-call(bf16[4,32,2048]{2,1,0:T(8,128)(2,1)} %bitcast.28, bf16[32,2048]{1,0:T(8,128)(2,1)} %bitcast.33, bf16[1,2048]{1,0:T(2,128)(2,1)} %reshape.74.gain, bf16[64,512]{1,0:T(8,128)(2,1)} %get-tuple-element.17.select), custom_call_target="tpu_custom_call" | custom-call | tf_op jit(solution)/shard_map/reduce_group/pallas_call | solution.py:334
  74.2 45.5 %dispatch.1 = bf16[2,4,32,8,1024]{4,3,2,1,0:T(8,128)(2,1)} custom-call(bf16[32,2,8,1024]{3,2,1,0:T(8,128)(2,1)} %get-tuple-element.18.packed), custom_call_target="tpu_custom_call" | custom-call | tf_op jit(solution)/shard_map/dispatch/pallas_call | solution.py:464
  119.7 1.6 copy.37
  121.3 1.6 copy.38
  122.9 1.0 copy.39.router
  123.9 13.4 %experts.1 = (bf16[2,1024,1024]{2,1,0:T(8,128)(2,1)}, bf16[2,64,512]{2,1,0:T(8,128)(2,1)}) custom-call(bf16[2,1024,1024]{2,1,0:T(8,128)(2,1)} %bitcast.22, bf16[2048,352]{1,0:T(8,128)(2,1)} %bitcast.23, bf16[2048,352]{1,0:T(8,128)(2,1)} %bitcast.24, bf16[352,2048]{1,0:T(8,128)(2,1)} %bitcast.30, bf16[64,2048]{1,0:T(8,128)(2,1)} %get-tuple-element.19.normed, ...), custom_call_target="tpu_custom_call" | custom-call | tf_op jit(solution)/shard_map/experts/pallas_call | solution.py:526
  137.3 1.3 copy.40.wl
  138.6 0.6 reshape.78.gain
  139.2 54.1 %combine.1 = (bf16[32,2048]{1,0:T(8,128)(2,1)}, bf16[4,32,768]{2,1,0:T(8,128)(2,1)}, bf16[4,32,144]{2,1,0:T(8,128)(2,1)}) custom-call(bf16[2,4,32,8,1024]{4,3,2,1,0:T(8,128)(2,1)} %bitcast.25, bf16[2,64,512]{2,1,0:T(8,128)(2,1)} %get-tuple-element.22.mix, bf16[32,2048]{1,0:T(8,128)(2,1)} %get-tuple-element.23.resid, bf16[1,2048]{1,0:T(2,128)(2,1)} %reshape.78.gain, ...), custom_call_target="tpu_custom_call" | custom-call | tf_op jit(solution)/shard_map/combine/pallas_call | solution.py:697
  193.3 1.1 copy.41
  194.4 0.7 reshape.80
  195.2 0.9 copy.42
  196.1 0.7 copy.43
  196.8 1.6 copy.48
  (21 shorter events, 0.6 us)
Async XLA Ops:
  0.6 0.7 copy-start
  0.6 5.5 %copy-start.6 = (bf16[128,576]{0,1:T(8,128)(2,1)S(1)}, bf16[128,576]{0,1:T(8,128)(2,1)}, u32[]{:S(2)}) copy-start(bf16[128,576]{0,1:T(8,128)(2,1)} %param.22) | copy-start | bytes 442372
  0.7 44.5 %copy-start.5 = (bf16[128,768]{1,0:T(8,128)(2,1)S(1)}, bf16[128,768]{1,0:T(8,128)(2,1)}, u32[]{:S(2)}) copy-start(bf16[128,768]{1,0:T(8,128)(2,1)} %param.21) | copy-start | bytes 589828
  46.2 14.9 %copy-start.7 = (bf16[2048]{0:T(1024)(128)(2,1)S(1)}, bf16[2048]{0:T(1024)(128)(2,1)}, u32[]{:S(2)}) copy-start(bf16[2048]{0:T(1024)(128)(2,1)} %param.27) | copy-start | bytes 12292
  74.2 45.6 %copy-start.1 = (bf16[1,2048,352]{1,2,0:T(8,128)(2,1)S(1)}, bf16[1,2048,352]{1,2,0:T(8,128)(2,1)}, u32[]{:S(2)}) copy-start(bf16[1,2048,352]{1,2,0:T(8,128)(2,1)} %param.29) | copy-start | bytes 4325380
  119.7 1.6 copy-start.2
  121.3 1.6 copy-start.4
  123.9 13.4 %copy-start.3 = (bf16[2048,144]{0,1:T(8,128)(2,1)S(1)}, bf16[2048,144]{0,1:T(8,128)(2,1)}, u32[]{:S(2)}) copy-start(bf16[2048,144]{0,1:T(8,128)(2,1)} %param.34) | copy-start | bytes 1769476
  123.9 14.7 %copy-start.8 = (bf16[2048]{0:T(1024)(128)(2,1)S(1)}, bf16[2048]{0:T(1024)(128)(2,1)}, u32[]{:S(2)}) copy-start(bf16[2048]{0:T(1024)(128)(2,1)} %param.32) | copy-start | bytes 12292

commit v2 on v0

v2 whole, which is shorter than its diff:
```python
import math
from types import SimpleNamespace

import jax
import jax.numpy as jnp
from jax import lax
from jax.experimental import pallas as pl
from jax.experimental.pallas import tpu as pltpu
from jax.sharding import PartitionSpec as P

NOPE = 128
ROPE = 64
LAT = 512
KEY = LAT + ROPE
PAGE = 8
REACH = 4
WIDTH = 2048
HALF = WIDTH // 2
EXPERTS = 64
TOP = 6
HEADS_DEV = 4
TOK = 128
QUARTER = 32
SLOTS = EXPERTS * 8
SCORE_SCALE = 1.0 / math.sqrt(NOPE + ROPE)
VERY_NEGATIVE = -1e30
ROUTE_SCALING = 2.446
NORM_EPSILON = 1e-06
BF16 = jnp.bfloat16
F32 = jnp.float32
MESH = pl.DeviceIdType.MESH
ANY = pl.BlockSpec(memory_space=pl.ANY)
VM = pl.BlockSpec(memory_space=pltpu.VMEM)
SM = pl.BlockSpec(memory_space=pltpu.SMEM)
DMA = pltpu.SemaphoreType.DMA
NT = (((1,), (1,)), ((), ()))
TN = (((0,), (0,)), ((), ()))


def coords():
    g = lax.axis_index("group")
    t = lax.axis_index("tensor")
    x = lax.div(g, 2) * 2 + lax.div(t, 32)
    y = lax.rem(lax.div(t, 8), 4)
    z = lax.rem(t, 8)
    return x, y, z, lax.rem(g, 2)


def group_of(x, c):
    return lax.div(x, 2) * 2 + c


def tensor_of(x, y, z):
    return (lax.rem(x, 2) * 4 + y) * 8 + z


def device(x, y, z, c):
    return {"group": group_of(x, c), "tensor": tensor_of(x, y, z)}


def remote(src, dst, send, recv, dev):
    return pltpu.make_async_remote_copy(
        src_ref=src, dst_ref=dst, send_sem=send, recv_sem=recv, device_id=dev, device_id_type=MESH
    )


def meet(peers):
    barrier = pltpu.get_barrier_semaphore()
    for peer in peers:
        pl.semaphore_signal(barrier, inc=1, device_id=peer, device_id_type=MESH)
    pl.semaphore_wait(barrier, len(peers))


def shape(dims, dtype=BF16):
    return jax.ShapeDtypeStruct(dims, dtype)


def iota(dims, axis):
    return lax.broadcasted_iota(jnp.int32, dims, axis)


def dot(a, b, dims=(((1,), (0,)), ((), ()))):
    return lax.dot_general(a, b, dims, preferred_element_type=F32)


def rows_at(start, size):
    return pl.ds(pl.multiple_of(start, size), size)


def normalized(values, gain):
    mean_square = jnp.sum(values * values, axis=-1, keepdims=True) * (1.0 / WIDTH)
    return (values * lax.rsqrt(mean_square + NORM_EPSILON) * gain.astype(F32)).astype(BF16)


def split_terms(values, count):
    terms = []
    for _ in range(count):
        term = values.astype(BF16)
        terms.append(term)
        values = values - term.astype(F32)
    return terms


def token_order():
    i, j = iota((TOK, TOK), 0), iota((TOK, TOK), 1)
    return (j == (i & 31) * 4 + (i >> 5)).astype(BF16)


def slot_spread():
    slot, e = iota((SLOTS, EXPERTS), 0), iota((SLOTS, EXPERTS), 1)
    return (e == ((slot >> 3) & 1) * 32 + (slot >> 4)).astype(BF16)


SPECS = dict(
    lens=SM, tenants=SM, spans=SM, pages=VM, routes=VM, queries=VM, suffix=VM, pref=VM,
    gain=VM, next_gain=VM,
    hidden_h=ANY, ku_h=ANY, vu_h=ANY, ow_h=ANY, gate_h=ANY, up_h=ANY, down_h=ANY,
    router_h=ANY, wq_h=ANY, wl_h=ANY,
)
LOADED = ("ku", "vu", "ow", "hidden", "router", "gate", "up", "down", "wq", "wl")
BLOCK = (8, HALF)
SCRATCH = dict(
    q=pltpu.VMEM((HEADS_DEV, TOK, NOPE + ROPE), BF16),
    ku=pltpu.VMEM((HEADS_DEV, NOPE, LAT), BF16),
    vu=pltpu.VMEM((HEADS_DEV, LAT, NOPE), BF16),
    ow=pltpu.VMEM((HEADS_DEV, NOPE, WIDTH), BF16),
    hidden=pltpu.VMEM((TOK, WIDTH), BF16),
    router=pltpu.VMEM((EXPERTS, WIDTH), BF16),
    gate=pltpu.VMEM((352, WIDTH), BF16),
    up=pltpu.VMEM((352, WIDTH), BF16),
    down=pltpu.VMEM((352, WIDTH), BF16),
    wq=pltpu.VMEM((WIDTH, 768), BF16),
    wl=pltpu.VMEM((144, WIDTH), BF16),
    load_sem=DMA((len(LOADED),)),
    zb=pltpu.VMEM((8, PAGE, KEY), BF16),
    pk=pltpu.VMEM((2048, KEY), BF16),
    sk=pltpu.VMEM((REACH * TOK, KEY), BF16),
    own=pltpu.VMEM((TOK, KEY), BF16),
    zs=DMA((8,)), zr=DMA((8,)),
    bs=DMA((4, 4)), br=DMA((4, 4)), cs=DMA((4, 4)), cr=DMA((4, 4)),
    us=DMA((REACH,)), ur=DMA((REACH,)), vs=DMA((REACH,)), vr=DMA((REACH,)),
    ws=DMA((REACH, 2)), wr=DMA((REACH, 2)),
    bias=pltpu.VMEM((TOK, 2688), F32),
    s=pltpu.VMEM((TOK, 2688), F32),
    acc=pltpu.VMEM((TOK, WIDTH), F32),
    att=pltpu.VMEM((4, QUARTER, WIDTH), BF16),
    near_a=pltpu.VMEM((2, QUARTER, WIDTH), BF16),
    half=pltpu.VMEM((QUARTER, WIDTH), BF16),
    far=pltpu.VMEM((QUARTER, WIDTH), BF16),
    resid=pltpu.VMEM((QUARTER, WIDTH), BF16),
    both=pltpu.VMEM((2, QUARTER, WIDTH), BF16),
    as_=DMA((2,)), ar=DMA((2,)), fs=DMA(()), fr=DMA(()), ts=DMA(()), tr=DMA(()),
    select=pltpu.VMEM((SLOTS, 64), BF16),
    member=pltpu.VMEM((EXPERTS, 64), F32),
    mix=pltpu.VMEM((2, SLOTS, 64), BF16),
    packed=pltpu.VMEM((32, 2) + BLOCK, BF16),
    land=pltpu.VMEM((32, 2) + BLOCK, BF16),
    rows=pltpu.VMEM((2, 4, 32) + BLOCK, BF16),
    parts=pltpu.VMEM((2, 4, 32) + BLOCK, BF16),
    d1s=DMA((32,)), d1r=DMA((32,)), d2s=DMA((4, 32)), d2r=DMA((4, 32)), d3s=DMA((4, 32)), d3r=DMA((4,)),
    near=pltpu.VMEM((4, 32) + BLOCK, BF16),
    summed=pltpu.VMEM((4, 32) + BLOCK, BF16),
    landed=pltpu.VMEM((4, 32) + BLOCK, BF16),
    turned=pltpu.VMEM((32, 2) + BLOCK, BF16),
    back=pltpu.VMEM((32, 2) + BLOCK, BF16),
    e1s=DMA((4, 4)), e1r=DMA((4, 4)), e2s=DMA((4, 4)), e2r=DMA((4, 4)), e3s=DMA((32,)), e3r=DMA((32,)),
    moe=pltpu.VMEM((2, QUARTER, HALF), F32),
    other=pltpu.VMEM((QUARTER, HALF), F32),
    normed=pltpu.VMEM((4, QUARTER, WIDTH), BF16),
    es=DMA(()), er=DMA(()), hs=DMA((3,)), hr=DMA((3,)),
)
OUTS = ("layer", "nq", "nl")


def layer_kernel(*refs):
    r = SimpleNamespace(**dict(zip(tuple(SPECS) + OUTS + tuple(SCRATCH), refs)))
    x, y, z, c = coords()
    g = lax.axis_index("group")
    t = lax.axis_index("tensor")
    xh, xl = lax.div(x, 2), lax.rem(x, 2)
    here = y * 8 + z
    sibling = device(x, y, z, 1 - c)
    x_dev = [None] + [device(lax.rem(x + d, 4), y, z, c) for d in range(1, 4)]
    ahead = [{"group": g, "tensor": lax.rem(t + k, 64)} for k in range(1, REACH + 1)]
    behind = [{"group": g, "tensor": lax.rem(t + 64 - k, 64)} for k in range(1, REACH + 1)]
    barrier = pltpu.get_barrier_semaphore()
    sends = []

    def go(src, dst, send, recv, dev):
        copy = remote(src, dst, send, recv, dev)
        copy.start()
        sends.append(copy)

    def yz(s, sign):
        dy, dz = lax.div(s, 8), lax.rem(s, 8)
        return lax.rem(y + 4 + sign * dy, 4), lax.rem(z + 8 + sign * dz, 8)

    def yz_index(s, sign):
        yy, zz = yz(s, sign)
        return yy * 8 + zz

    def yz_dev(s, sign):
        yy, zz = yz(s, sign)
        return device(x, yy, zz, c)

    def greet(s, _):
        pl.semaphore_signal(barrier, inc=1, device_id=yz_dev(s, 1), device_id_type=MESH)
        return 0

    lax.fori_loop(1, 32, greet, 0)
    peers = x_dev[1:] + [sibling] + ahead + behind
    for peer in peers:
        pl.semaphore_signal(barrier, inc=1, device_id=peer, device_id_type=MESH)
    loads = {}
    for i, name in enumerate(LOADED):
        loads[name] = pltpu.make_async_copy(
            getattr(r, name + "_h"), getattr(r, name), r.load_sem.at[i]
        )
        loads[name].start()
    eye = (iota((TOK, TOK), 0) == iota((TOK, TOK), 1)).astype(BF16)
    r.own[...] = dot(eye, r.suffix[...], NT).astype(BF16)
    r.zb[z] = r.pref[...]
    for h in range(HEADS_DEV):
        r.q[h] = r.queries[:, h * (NOPE + ROPE) : (h + 1) * (NOPE + ROPE)]

    first = t * TOK
    pos = first + iota((TOK, 1), 0)

    def one_request(i, state):
        start, begin, low, high = state
        end = start + r.lens[i]
        inside = (pos >= start) & (pos < end)
        tenant = r.tenants[i]
        lo = jnp.int32(0)
        hi = r.spans[0]
        for k in range(3):
            more = tenant > k
            lo = lo + jnp.where(more, r.spans[k], 0)
            hi = hi + jnp.where(more, r.spans[k + 1], 0)
        begin = jnp.where(inside, start, begin)
        low = jnp.where(inside, lo, low)
        high = jnp.where(inside, hi, high)
        return end, begin, low, high

    zero = jnp.zeros((TOK, 1), jnp.int32)
    _, begin, low, high = lax.fori_loop(0, 32, one_request, (jnp.int32(0), zero, zero, zero))
    page, spot = iota((256, 2048), 0), iota((256, 2048), 1)
    expand = (page == (spot >> 3)).astype(BF16)
    table = jnp.broadcast_to(r.pages[...], (8, 256)).astype(F32).astype(BF16)
    logical = dot(table, expand)[0:1].astype(jnp.int32) * PAGE + (iota((1, 2048), 1) & 7)
    seen = (logical >= low) & (logical < high)
    r.bias[:, 0:2048] = jnp.where(seen, 0.0, VERY_NEGATIVE)
    col = iota((1, 640), 1)
    step = col >> 7
    spot = first + (col & 127) - jnp.where(step == 4, 0, (step + 1) * TOK)
    seen = (spot >= begin) & (spot <= pos)
    r.bias[:, 2048:2688] = jnp.where(seen, 0.0, VERY_NEGATIVE)

    pl.semaphore_wait(barrier, 31 + len(peers))

    z_dev = [None] + [device(x, y, lax.rem(z + d, 8), c) for d in range(1, 8)]
    p_dev = [None] + [
        device(lax.rem(x + d * c, 4), lax.rem(y + d * (1 - c), 4), z, c) for d in range(1, 4)
    ]
    q_dev = [None] + [
        device(lax.rem(x + d * (1 - c), 4), lax.rem(y + d * c, 4), z, c) for d in range(1, 4)
    ]

    def block(dp, dq, core):
        bx = lax.rem(x + 8 - dp * core - dq * (1 - core), 4)
        by = lax.rem(y + 8 - dp * (1 - core) - dq * core, 4)
        return r.pk.at[rows_at((group_of(bx, core) * 64 + tensor_of(bx, by, 0)) * PAGE, 64)]

    def near_rows(k, who):
        return r.sk.at[rows_at((k * 4 + who) * QUARTER, QUARTER)]

    for d in range(1, 8):
        go(r.zb.at[z], r.zb.at[z], r.zs.at[d], r.zr.at[d], z_dev[d])
    for k in range(REACH):
        go(r.own.at[rows_at(g * QUARTER, QUARTER)], near_rows(k, g), r.us.at[k], r.ur.at[k], ahead[k])

    hit = jnp.zeros((EXPERTS, 64), F32)
    for k in range(TOP):
        pair = jnp.where(xh == 0, r.routes[k, 0:2, :], r.routes[k, 2:4, :])
        line = jnp.concatenate([pair[0:1], pair[1:2]], axis=1)
        hit = hit + (line == iota((EXPERTS, 64), 0)).astype(F32)
    r.member[...] = hit
    i, j = iota((64, 64), 0), iota((64, 64), 1)
    before = ((i < j) & ((i >> 5) == (j >> 5))).astype(BF16)
    rank = dot(hit.astype(BF16), before)
    spread = slot_spread()
    hit_wide = dot(spread, hit.astype(BF16))
    rank_wide = dot(spread, rank.astype(BF16))
    slot, token = iota((SLOTS, 64), 0), iota((SLOTS, 64), 1)
    chosen = (hit_wide > 0.5) & (rank_wide == (slot & 3).astype(F32))
    chosen = chosen & (((slot >> 2) & 1) == (token >> 5))
    r.select[...] = chosen.astype(BF16)

    for d in range(1, 8):
        row = r.zb.at[lax.rem(z + 8 - d, 8)]
        remote(row, row, r.zs.at[d], r.zr.at[d], sibling).wait_recv()
    own_rows = rows_at((g * 64 + tensor_of(x, y, 0)) * PAGE, 64)
    r.pk[own_rows] = r.zb[...].reshape(64, KEY)
    start = block(0, 0, c)
    for d in range(1, 4):
        go(start, start, r.bs.at[d, 0], r.br.at[d, 0], p_dev[d])
    for d in range(1, 4):
        go(start, start, r.bs.at[0, d], r.br.at[0, d], q_dev[d])
    go(start, start, r.cs.at[0, 0], r.cr.at[0, 0], sibling)
    for dp in range(1, 4):
        spot = block(dp, 0, c)
        remote(spot, spot, r.bs.at[dp, 0], r.br.at[dp, 0], sibling).wait_recv()
        for d in range(1, 4):
            go(spot, spot, r.bs.at[dp, d], r.br.at[dp, d], q_dev[d])
        go(spot, spot, r.cs.at[dp, 0], r.cr.at[dp, 0], sibling)
    for k in range(REACH):
        spot = near_rows(k, g)
        remote(spot, spot, r.us.at[k], r.ur.at[k], sibling).wait_recv()
        go(spot, spot, r.vs.at[k], r.vr.at[k], x_dev[2])
        go(spot, spot, r.ws.at[k, 0], r.wr.at[k, 0], sibling)
    for dp in range(4):
        for dq in range(1, 4):
            spot = block(dp, dq, c)
            remote(spot, spot, r.bs.at[dp, dq], r.br.at[dp, dq], sibling).wait_recv()
            go(spot, spot, r.cs.at[dp, dq], r.cr.at[dp, dq], sibling)
    far_g = lax.rem(g + 2, 4)
    gs = g + 1 - 2 * c
    far_s = lax.rem(gs + 2, 4)
    for k in range(REACH):
        spot = near_rows(k, far_g)
        remote(spot, spot, r.vs.at[k], r.vr.at[k], sibling).wait_recv()
        go(spot, spot, r.ws.at[k, 1], r.wr.at[k, 1], sibling)
    for dp in range(4):
        for dq in range(4):
            spot = block(dp, dq, 1 - c)
            remote(spot, spot, r.cs.at[dp, dq], r.cr.at[dp, dq], sibling).wait_recv()
    for k in range(REACH):
        for side, who in ((0, gs), (1, far_s)):
            spot = near_rows(k, who)
            remote(spot, spot, r.ws.at[k, side], r.wr.at[k, side], sibling).wait_recv()

    for name in ("ku", "vu", "ow"):
        loads[name].wait()
    r.acc[...] = jnp.zeros_like(r.acc)
    order = token_order()

    def one_head(h, _):
        qh = r.q[h]
        absorbed = dot(qh[:, :NOPE], r.ku[h]).astype(BF16)
        full = jnp.concatenate([absorbed, qh[:, NOPE:]], axis=1)
        pieces = ((r.pk, 0, 2048), (r.sk, 2048, 2560), (r.own, 2560, 2688))
        for keys, lo, hi in pieces:
            r.s[:, lo:hi] = dot(full, keys[...], NT) * SCORE_SCALE + r.bias[:, lo:hi]
        best = jnp.max(r.s[...], axis=1, keepdims=True)
        total = jnp.zeros((TOK, 1), F32)
        mixed = jnp.zeros((TOK, LAT), F32)
        for keys, lo, hi in pieces:
            weights = jnp.exp(r.s[:, lo:hi] - best)
            total = total + jnp.sum(weights, axis=1, keepdims=True)
            mixed = mixed + dot(weights.astype(BF16), keys[:, :LAT])
        latent = (mixed / total).astype(BF16)
        head = dot(latent, r.vu[h]).astype(BF16)
        head = dot(order, head).astype(BF16)
        r.acc[...] += dot(head, r.ow[h])
        return 0

    lax.fori_loop(0, HEADS_DEV, one_head, 0)
    r.att[...] = r.acc[...].astype(BF16).reshape(4, QUARTER, WIDTH)

    for k in range(2):
        go(r.att.at[2 * k + 1 - c], r.near_a.at[k], r.as_.at[k], r.ar.at[k], sibling)
    loads["hidden"].wait()
    mine_rows = (iota((QUARTER, TOK), 1) == iota((QUARTER, TOK), 0) * 4 + g).astype(BF16)
    hq = dot(mine_rows, r.hidden[...])
    for k in range(2):
        remote(r.near_a.at[k], r.near_a.at[k], r.as_.at[k], r.ar.at[k], sibling).wait_recv()
    r.half[...] = (r.att[2 * (1 - xh) + c].astype(F32) + r.near_a[1 - xh].astype(F32)).astype(BF16)
    go(r.half, r.far, r.fs, r.fr, x_dev[2])
    mine = r.att[2 * xh + c].astype(F32) + r.near_a[xh].astype(F32) + hq
    gain = r.gain[...].reshape(1, WIDTH)
    next_gain = r.next_gain[...].reshape(1, WIDTH)
    remote(r.half, r.far, r.fs, r.fr, x_dev[2]).wait_recv()
    residual = (mine + r.far[...].astype(F32)).astype(BF16)
    r.resid[...] = residual
    r.both[c] = normalized(residual.astype(F32), gain)
    go(r.both.at[c], r.both.at[c], r.ts, r.tr, sibling)
    remote(r.both.at[1 - c], r.both.at[1 - c], r.ts, r.tr, sibling).wait_recv()
    part = r.both[:, :, rows_at(c * HALF, HALF)].reshape(64, HALF)
    r.packed[...] = dot(r.select[...], part).astype(BF16).reshape((32, 2) + BLOCK)

    def first_leg(s):
        return remote(r.packed.at[yz_index(s, 1)], r.land.at[here], r.d1s.at[s], r.d1r.at[s], yz_dev(s, 1))

    def x_leg(s, d, src):
        spot = r.rows.at[c, x, yz_index(s, -1)]
        return remote(src, spot, r.d2s.at[d, s], r.d2r.at[d, s], x_dev[d])

    def to_sibling(s, d, src):
        spot = r.rows.at[c, lax.rem(x + d, 4), yz_index(s, -1)]
        return remote(src, spot, r.d3s.at[d, s], r.d3r.at[lax.div(s, 8)], sibling)

    def start_first(s, _):
        first_leg(s).start()
        return 0

    lax.fori_loop(1, 32, start_first, 0)
    r.land[here] = r.packed[here]

    def forward(s, _):
        block = yz_index(s, -1)

        @pl.when(s >= 1)
        def _():
            spot = r.land.at[block]
            remote(spot, spot, r.d1s.at[s], r.d1r.at[s], sibling).wait_recv()

        same, cross = r.land.at[block, xl], r.land.at[block, 1 - xl]
        x_leg(s, 2, same).start()
        x_leg(s, 1, cross).start()
        x_leg(s, 3, cross).start()
        to_sibling(s, 0, same).start()
        r.rows[c, x, block] = r.land[block, xl]
        return 0

    def pass_on(s, _):
        for d in (1, 3, 2):
            spot = r.rows.at[c, lax.rem(x + d, 4), yz_index(s, -1)]
            remote(spot, spot, r.d2s.at[4 - d, s], r.d2r.at[4 - d, s], sibling).wait_recv()
            to_sibling(s, d, spot).start()
        return 0

    def span(k):
        return rows_at(lax.rem(y + 4 - k, 4) * 8, 8)

    def near_copy(k, d):
        xd = lax.rem(x + d, 4)
        return remote(
            r.parts.at[1 - c, xd, span(k)], r.near.at[xd, span(k)], r.e1s.at[k, d], r.e1r.at[k, d], sibling
        )

    def x_copy(k, d):
        xd = lax.rem(x + d, 4)
        return remote(
            r.summed.at[xd, span(k)], r.landed.at[d, span(k)], r.e2s.at[k, d], r.e2r.at[k, d], x_dev[d]
        )

    def back_copy(s):
        return remote(r.turned.at[yz_index(s, -1)], r.back.at[here], r.e3s.at[s], r.e3r.at[s], yz_dev(s, -1))

    turn_order = (2, 1, 3, 0)

    def expert(k):
        spot = r.rows.at[1 - c, :, span(k)]
        remote(spot, spot, r.d3s.at[0, 0], r.d3r.at[k], sibling).wait_recv()
        left = r.rows[0, :, span(k)].reshape(256, HALF)
        right = r.rows[1, :, span(k)].reshape(256, HALF)
        gate_vals = dot(left, r.gate[:, :HALF], NT) + dot(right, r.gate[:, HALF:], NT)
        up_vals = dot(left, r.up[:, :HALF], NT) + dot(right, r.up[:, HALF:], NT)
        hidden = (gate_vals / (1.0 + jnp.exp(-gate_vals)) * up_vals).astype(BF16)
        for side in range(2):
            result = dot(hidden, r.down[:, side * HALF : (side + 1) * HALF]).astype(BF16)
            r.parts[side, :, span(k)] = result.reshape((4, 8) + BLOCK)
        for d in turn_order:
            near_copy(k, d).start()

    def sum_near(k):
        for d in turn_order:
            near_copy(k, d).wait_recv()
            xd = lax.rem(x + d, 4)
            total = r.parts[c, xd, span(k)].astype(F32) + r.near[xd, span(k)].astype(F32)
            r.summed[xd, span(k)] = total.astype(BF16)
            if d > 0:
                x_copy(k, d).start()

    loads["router"].wait()
    logits = dot(r.router[...], r.both[...].reshape(64, WIDTH), NT)
    picked = jax.nn.sigmoid(logits) * r.member[...]
    weights = picked / jnp.sum(picked, axis=0, keepdims=True) * ROUTE_SCALING
    wide = jnp.zeros((SLOTS, 64), F32)
    spread = slot_spread()
    for term in split_terms(weights, 3):
        wide = wide + dot(spread, term)
    wide = wide * r.select[...].astype(F32)
    for k, term in enumerate(split_terms(wide, 2)):
        r.mix[k] = term
    for name in ("gate", "up", "down"):
        loads[name].wait()

    def stage(k, _):
        lax.fori_loop(k * 8, k * 8 + 8, forward, 0)

        @pl.when(k >= 2)
        def _():
            expert(k - 2)

        @pl.when(k >= 3)
        def _():
            sum_near(k - 3)

        @pl.when(k >= 1)
        def _():
            lax.fori_loop(k * 8 - 8, k * 8, pass_on, 0)

        return 0

    lax.fori_loop(0, 4, stage, 0)

    def late(k, _):
        expert(k)
        sum_near(k - 1)

        @pl.when(k == 2)
        def _():
            lax.fori_loop(24, 32, pass_on, 0)

        return 0

    lax.fori_loop(2, 4, late, 0)
    sum_near(3)

    def sum_x(k, _):
        for d in range(1, 4):
            x_copy(k, d).wait_recv()
        same = r.summed[x, span(k)].astype(F32) + r.landed[2, span(k)].astype(F32)
        cross = r.landed[1, span(k)].astype(F32) + r.landed[3, span(k)].astype(F32)
        r.turned[span(k), xl] = same.astype(BF16)
        r.turned[span(k), 1 - xl] = cross.astype(BF16)
        for n in range(8):
            s = k * 8 + n

            @pl.when(s >= 1)
            def _():
                back_copy(s).start()

        return 0

    lax.fori_loop(0, 4, sum_x, 0)
    r.back[here] = r.turned[here]

    def arrive(s, _):
        spot = r.back.at[yz_index(s, 1)]
        remote(spot, spot, r.e3s.at[s], r.e3r.at[s], sibling).wait_recv()
        return 0

    lax.fori_loop(1, 32, arrive, 0)
    values = r.back[...].reshape(SLOTS, HALF)
    gated = dot(r.mix[0], values, TN) + dot(r.mix[1], values, TN)
    r.moe[...] = gated.reshape(2, QUARTER, HALF)
    go(r.moe.at[1 - c], r.other, r.es, r.er, sibling)
    my_cols, their_cols = rows_at(c * HALF, HALF), rows_at((1 - c) * HALF, HALF)
    r.layer[:, my_cols] = (r.resid[:, my_cols].astype(F32) + r.moe[c]).astype(BF16)
    remote(r.moe.at[1 - c], r.other, r.es, r.er, sibling).wait_recv()
    r.layer[:, their_cols] = (r.resid[:, their_cols].astype(F32) + r.other[...]).astype(BF16)
    r.normed[g] = normalized(r.layer[...].astype(F32), next_gain)

    def share(k, who, dev):
        return remote(r.normed.at[who], r.normed.at[who], r.hs.at[k], r.hr.at[k], dev)

    share(0, g, x_dev[2]).start()
    share(1, g, sibling).start()
    loads["wq"].wait()
    loads["wl"].wait()
    share(0, far_g, sibling).wait_recv()
    share(2, far_g, sibling).start()
    share(1, gs, sibling).wait_recv()
    share(2, far_s, sibling).wait_recv()
    block = dot(order, r.normed[...].reshape(TOK, WIDTH), TN).astype(BF16)
    r.nq[...] = dot(block, r.wq[...]).astype(BF16)
    r.nl[...] = dot(r.wl[...], block, NT).astype(BF16)

    for copy in sends:
        copy.wait_send()
    share(0, g, x_dev[2]).wait_send()
    share(1, g, sibling).wait_send()
    share(2, far_g, sibling).wait_send()

    def drain(s, _):
        for d in range(1, 4):
            x_leg(s, d, r.land.at[0, 0]).wait_send()
        for d in range(4):
            to_sibling(s, d, r.land.at[0, 0]).wait_send()

        @pl.when(s >= 1)
        def _():
            first_leg(s).wait_send()
            back_copy(s).wait_send()

        return 0

    lax.fori_loop(0, 32, drain, 0)

    def drain_chunks(k, _):
        for d in turn_order:
            near_copy(k, d).wait_send()
            if d > 0:
                x_copy(k, d).wait_send()
        return 0

    lax.fori_loop(0, 4, drain_chunks, 0)


def whole_layer(**operands):
    return pl.pallas_call(
        layer_kernel,
        out_shape=(shape((QUARTER, WIDTH)), shape((TOK, 768)), shape((144, TOK))),
        in_specs=list(SPECS.values()),
        out_specs=(VM, VM, VM),
        scratch_shapes=list(SCRATCH.values()),
        compiler_params=pltpu.CompilerParams(
            collective_id=0, has_side_effects=True, vmem_limit_bytes=60 << 20
        ),
        name="layer",
    )(*[operands[name] for name in SPECS])


def per_device(
    hidden_in,
    queries,
    suffix_latent,
    prefix_latent,
    key_up,
    value_up,
    output_weight,
    norm_gain,
    router,
    expert_gate,
    expert_up,
    expert_down,
    next_gain,
    next_query_weight,
    next_latent_weight,
    suffix_lengths,
    request_tenant,
    tenant_lengths,
    page_table,
    routes,
):
    layer, nq, nl = whole_layer(
        lens=suffix_lengths,
        tenants=request_tenant,
        spans=tenant_lengths,
        pages=page_table.reshape(1, -1),
        routes=routes.transpose(2, 0, 1),
        queries=queries,
        suffix=suffix_latent.T,
        pref=prefix_latent,
        gain=norm_gain,
        next_gain=next_gain,
        hidden_h=hidden_in,
        ku_h=key_up,
        vu_h=value_up,
        ow_h=output_weight.reshape(HEADS_DEV, NOPE, WIDTH),
        gate_h=expert_gate[0].T,
        up_h=expert_up[0].T,
        down_h=expert_down[0],
        router_h=router.T,
        wq_h=next_query_weight,
        wl_h=next_latent_weight.T,
    )
    return layer.reshape(QUARTER, 1, WIDTH), nq, nl.T


def solution(mesh):
    return jax.shard_map(
        per_device,
        mesh=mesh,
        in_specs=(
            P("tensor", None),
            P("tensor", "group"),
            P("tensor", None),
            P(("group", "tensor"), None),
            P("group", None, None),
            P("group", None, None),
            P("group", None),
            P(),
            P(),
            P("tensor", None, "group"),
            P("tensor", None, "group"),
            P("tensor", "group", None),
            P(),
            P(None, "group"),
            P(None, "group"),
            P(),
            P(),
            P(),
            P(),
            P(None, "tensor", None),
        ),
        out_specs=(P("tensor", "group", None), P("tensor", "group"), P("tensor", "group")),
        check_vma=False,
    )
```

time: 1170 us -> 143 us (0.12)
  waiting for transfers between devices: 888 us -> 0 us
  Pallas kernels: 0 us -> 138 us
  blocking collectives: 113 us -> 0 us
  local copies, waits for them, and re-layouts: 63.8 us -> 4.57 us
  matrix products: 33.6 us -> 0 us
  starting transfers between devices: 28.4 us -> 0 us
  other arithmetic: 26.9 us -> 0 us
  between operations: 17.6 us -> 0.65 us
    all_gather x1 -> x0, waiting for transfers between devices: 674 us -> none  [per_device(): lax.all_gather(prefix_latent, ('group', 'tensor'), axis=0, tiled=True)]
    pallas_call x0 -> x1, Pallas kernels: none -> 138 us  [whole_layer(): pl.pallas_call(layer_kernel, out_shape=(shape((QUARTER, WIDTH)), shape((T...]
    all_to_all x1 -> x0, blocking collectives: 104 us -> none  [per_device(): lax.all_to_all(outgoing, 'tensor', split_axis=0, concat_axis=0, tiled=True)]
    psum x1 -> x0, waiting for transfers between devices: 99.8 us -> none  [per_device(): lax.psum(attend_part.astype(jnp.bfloat16), 'group').astype(jnp.float32)]
    all_to_all x1 -> x0, waiting for transfers between devices: 82.8 us -> none  [per_device(): lax.all_to_all(partials, 'tensor', split_axis=0, concat_axis=0, tiled=True)]
    dot_general x13 -> x0, matrix products: 33.6 us -> none  [the longest x1 9.36 us: expert_apply(): jnp.dot(hidden_vals, down_part, preferred_element_type=jnp.float32)]
    reduce_scatter x1 -> x0, waiting for transfers between devices: 31.3 us -> none  [per_device(): lax.psum_scatter(moe_part.reshape(tok_quarter, groups, width).astype(jnp....]
    gather x8 -> x0, local copies, waits for them, and re-layouts: 21.8 us -> none  [the longest x2 16.1 us: per_device(): picked = jnp.take(returned, targets, axis=0)]
  transfers between devices with their start and end apart: 8 -> 0, of which waited for: 4 -> 0; matrix products, arithmetic and copies ran while one was open for 6% -> 0% of each run, Pallas kernels for 0% -> 0%
where the time goes in v2:
time: 143 us
  Pallas kernels  138 us (97%)
  local copies, waits for them, and re-layouts  4.57 us (3%)
    pallas_call x1, Pallas kernels, whole_layer(): pl.pallas_call(layer_kernel, out_shape=(shape((QUARTER, WIDTH)), shape((T...  138 us
    unnamed x3, local copies, waits for them, and re-layouts  4.57 us

profile of v2, /device:TPU:1, one launch (start us, length us, event | category | flops | bytes accessed | tf_op | source)
XLA Modules:
  0.0 142.8 jit_solution(6397614844008924639)
XLA Ops:
  0.6 137.6 %layer.1 = (bf16[32,2048]{1,0:T(8,128)(2,1)}, bf16[128,768]{1,0:T(8,128)(2,1)}, bf16[144,128]{1,0:T(8,128)(2,1)}) custom-call(s32[32]{0:T(128)} %refs_0_.1, s32[32]{0:T(128)} %refs_1_.1, s32[4]{0:T(128)} %refs_2_.1, s32[1,256]{1,0:T(1,128)} %bitcast.25, s32[6,4,32]{2,1,0:T(4,128)} %bitcast.24, bf16[128,768]{1,0:T(8,128)(2,1)} %refs_5_.1, ...), custom_call_target="tpu_custom_call" | custom-call | tf_op jit(solution)/shard_map/layer/pallas_call | solution.py:603
  138.2 1.6 %copy.26 = bf16[32,1,2048]{2,0,1:T(8,128)(2,1)} copy(bf16[32,1,2048]{2,0,1:T(8,128)(2,1)} %bitcast.22) | data formatting | bytes 262144
  139.8 1.6 %copy.27 = bf16[128,768]{1,0:T(8,128)(2,1)} copy(bf16[128,768]{1,0:T(8,128)(2,1)} %get-tuple-element.13) | data formatting | bytes 393216
  141.4 1.4 copy.28
